TPU v7x, 1024 devices: a whole 4x4x32 slice. The times are simulated.
1024 devices in a mesh: dp: 2 (over core), ctx: 128 (over z, x), tp: 4 (over y).
Axes of the slice: x: 4, y: 4, z: 32, core: 2. Of those that a mesh axis runs over, the one named last changes fastest.
Arguments:
- queries: bfloat16 [2, 16384, 2048], P('dp', 'ctx', 'tp'), may hold values from -48 to 48
- key_rows: bfloat16 [2, 16384, 1024], P('dp', 'ctx', 'tp'), may hold values from -6 to 6
- values: bfloat16 [2, 16384, 1024], P('dp', 'ctx', 'tp'), may hold values from -6 to 6
- grad_out: bfloat16 [2, 16384, 2048], P('dp', 'ctx', 'tp'), may hold values from -6 to 6
- lengths: int32 [2, 8], replicated, may hold values from 1 to 8192, 16384 in all within a row
- pair_swap: int32 [128], P('ctx'), may hold values from 0 to 1
Outputs:
- attn_out: bfloat16 [2, 16384, 2048], P('dp', ('ctx', 'tp'))
- grad_query: bfloat16 [2, 16384, 2048], P('dp', 'ctx', 'tp')
- grad_keys: bfloat16 [2, 16384, 1024], P('dp', 'ctx', 'tp')
- grad_values: bfloat16 [2, 16384, 1024], P('dp', 'ctx', 'tp')
All inputs are finite; a program needn't handle non-finite values.
Results may differ from a plain program's by a relative error of at most 0.012.
Values may be sent and summed in bfloat16 or wider, within the bound.
A program may use at most 32 MiB of HBM per device.

v0:
```python
import jax
import jax.numpy as jnp
from jax import lax
from jax.sharding import PartitionSpec as P

HD = 128
REP = 2
W = 512


SCALE = 168.0 ** (-0.5)
NEGATIVE = -1e30


def from_partner(block, axis, apart):
    count = lax.axis_size(axis)
    route = []
    for low in range(count):
        high = low | 1 << apart
        if high != low and high < count:
            route += [(low, high), (high, low)]
    return lax.ppermute(block, axis, route)


def from_behind(block, axis, distance):
    devices = range(lax.axis_size(axis))
    route = [(i - distance, i) for i in devices if i - distance in devices]
    return lax.ppermute(block, axis, route)


def window_mask(start_pos, row_count, key_count, run_ends):
    q_pos = start_pos + jnp.arange(row_count, dtype=jnp.int32)
    k_pos = start_pos - (key_count - row_count) + jnp.arange(key_count, dtype=jnp.int32)
    q_seg = jnp.sum((q_pos[:, None] >= run_ends[None, :]).astype(jnp.int32), axis=1)
    k_seg = jnp.sum((k_pos[:, None] >= run_ends[None, :]).astype(jnp.int32), axis=1)
    spacing = q_pos[:, None] - k_pos[None, :]
    return (
        (spacing >= 0) & (spacing < W) & (k_pos[None, :] >= 0) & (q_seg[:, None] == k_seg[None, :])
    )


def group_core(q_part, k_part, v_part, g_part, allowed, repeat):
    row_count = q_part.shape[0]
    width = k_part.shape[1]
    q_heads = q_part.reshape(row_count, repeat, width)
    g_heads = g_part.reshape(row_count, repeat, width)
    scores = jnp.einsum("qrd,kd->rqk", q_heads, k_part, preferred_element_type=jnp.float32) * SCALE
    scores = jnp.where(allowed[None], scores, NEGATIVE)
    row_peak = jnp.max(scores, axis=2, keepdims=True)
    weights = jnp.exp(scores - row_peak)
    probs = weights / jnp.sum(weights, axis=2, keepdims=True)
    probs_low = probs.astype(jnp.bfloat16)
    attended = (
        jnp.einsum("rqk,kd->qrd", probs_low, v_part, preferred_element_type=jnp.float32)
        .astype(jnp.bfloat16)
        .reshape(row_count, repeat * width)
    )
    dprob = jnp.einsum("qrd,kd->rqk", g_heads, v_part, preferred_element_type=jnp.float32)
    delta = jnp.sum(probs * dprob, axis=2, keepdims=True)
    dscore = (probs * (dprob - delta)).astype(jnp.bfloat16)
    grad_q = (
        (jnp.einsum("rqk,kd->qrd", dscore, k_part, preferred_element_type=jnp.float32) * SCALE)
        .astype(jnp.bfloat16)
        .reshape(row_count, repeat * width)
    )
    grad_k = jnp.einsum("rqk,qrd->kd", dscore, q_heads, preferred_element_type=jnp.float32) * SCALE
    grad_v = jnp.einsum("rqk,qrd->kd", probs_low, g_heads, preferred_element_type=jnp.float32)
    return (attended, grad_q, grad_k, grad_v)


def attend_groups(q_part, k_part, v_part, g_part, allowed):
    group_count = k_part.shape[1] // HD
    pieces = []
    for group_idx in range(group_count):
        q_cols = slice(group_idx * REP * HD, (group_idx + 1) * REP * HD)
        k_cols = slice(group_idx * HD, (group_idx + 1) * HD)
        pieces.append(
            group_core(
                q_part[:, q_cols],
                k_part[:, k_cols],
                v_part[:, k_cols],
                g_part[:, q_cols],
                allowed,
                REP,
            )
        )
    return tuple(
        (jnp.concatenate([piece[member] for piece in pieces], axis=1) for member in range(4))
    )


def body(queries, key_rows, values, grad_out, lengths, pair_swap):
    flipped = pair_swap[0] == 1
    stored = (queries[0], key_rows[0], values[0], grad_out[0])
    partner = from_partner((queries[0], key_rows[0], values[0], grad_out[0]), "dp", 0)
    q_own, k_own, v_own, g_own = [
        jnp.where(flipped, other, mine) for mine, other in zip(stored, partner)
    ]
    row_count = q_own.shape[0]
    reach = W // row_count
    pack_idx = lax.axis_index("dp")
    run_ends = jnp.cumsum(lax.dynamic_index_in_dim(lengths, pack_idx, 0, keepdims=False))
    start_pos = lax.axis_index("ctx") * row_count
    earlier = [from_behind((k_own, v_own), "ctx", distance) for distance in range(reach, 0, -1)]
    window_keys = jnp.concatenate([item[0] for item in earlier] + [k_own], axis=0)
    window_values = jnp.concatenate([item[1] for item in earlier] + [v_own], axis=0)
    allowed = window_mask(start_pos, row_count, window_keys.shape[0], run_ends)
    attended, grad_q, partial_k, partial_v = attend_groups(
        q_own, window_keys, window_values, g_own, allowed
    )
    own_k = partial_k[reach * row_count :]
    own_v = partial_v[reach * row_count :]
    for distance in range(1, reach + 1):
        begin = (reach - distance) * row_count
        got_k, got_v = from_behind(
            (partial_k[begin : begin + row_count], partial_v[begin : begin + row_count]),
            "ctx",
            -distance,
        )
        own_k = own_k + got_k
        own_v = own_v + got_v
    token_rows = lax.all_to_all(attended, "tp", split_axis=0, concat_axis=1, tiled=True)
    return (
        token_rows[None],
        grad_q[None],
        own_k.astype(jnp.bfloat16)[None],
        own_v.astype(jnp.bfloat16)[None],
    )


def solution(mesh):
    placed = (
        P("dp", "ctx", "tp"),
        P("dp", "ctx", "tp"),
        P("dp", "ctx", "tp"),
        P("dp", "ctx", "tp"),
        P(),
        P("ctx"),
    )
    return jax.shard_map(
        body,
        mesh=mesh,
        in_specs=placed,
        out_specs=(
            P("dp", ("ctx", "tp"), None),
            P("dp", "ctx", "tp"),
            P("dp", "ctx", "tp"),
            P("dp", "ctx", "tp"),
        ),
        check_vma=False,
    )
```

profile of v0, /device:TPU:648, one launch (start us, length us, event | category | flops | bytes accessed | tf_op | source)
XLA Modules:
  0.0 107.6 jit_solution(2282610568181426504)
XLA Ops:
  0.6 0.0 copy-start
  0.6 1.9 %collective-permute-start = (bf16[128,256]{1,0:T(8,128)(2,1)}, bf16[128,256]{1,0:T(8,128)(2,1)S(1)}, u32[]{:S(2)}, u32[]{:S(2)}) collective-permute-start(bf16[128,256]{1,0:T(8,128)(2,1)} %bitcast.166), channel_id=1, source_target_pairs={{0,512},{512,0},{1,513},{513,1},{2,514},{514,2},{3,515},{515,3},{4... | collective-permute-start | bytes 196616 | tf_op jit(solution)/shard_map/ppermute | solution.py:22
  2.6 2.5 %collective-permute-start.5 = (bf16[128,256]{1,0:T(8,128)(2,1)}, bf16[128,256]{1,0:T(8,128)(2,1)S(1)}, u32[]{:S(2)}, u32[]{:S(2)}) collective-permute-start(bf16[128,256]{1,0:T(8,128)(2,1)} %bitcast.167), channel_id=1, source_target_pairs={{0,512},{512,0},{1,513},{513,1},{2,514},{514,2},{3,515},{515,3},{4... | collective-permute-start | bytes 196616 | tf_op jit(solution)/shard_map/ppermute | solution.py:22
  5.1 1.0 copy.90
  6.2 1.9 %collective-permute-start.11 = (bf16[128,512]{0,1:T(8,128)(2,1)S(1)}, bf16[128,512]{0,1:T(8,128)(2,1)S(1)}, u32[]{:S(2)}, u32[]{:S(2)}) collective-permute-start(bf16[128,512]{0,1:T(8,128)(2,1)S(1)} %bitcast.154), channel_id=1, source_target_pairs={{0,512},{512,0},{1,513},{513,1},{2,514},{514,2},{3,515},{515,3},{4... | collective-permute-start | bytes 393224 | tf_op jit(solution)/shard_map/ppermute | solution.py:22
  8.1 0.1 copy.80
  8.2 2.4 %collective-permute-start.10 = (bf16[128,512]{0,1:T(8,128)(2,1)S(1)}, bf16[128,512]{0,1:T(8,128)(2,1)S(1)}, u32[]{:S(2)}, u32[]{:S(2)}) collective-permute-start(bf16[128,512]{0,1:T(8,128)(2,1)S(1)} %bitcast.155), channel_id=1, source_target_pairs={{0,512},{512,0},{1,513},{513,1},{2,514},{514,2},{3,515},{515,3},{4... | collective-permute-start | bytes 393224 | tf_op jit(solution)/shard_map/ppermute | solution.py:22
  10.7 0.0 copy-start.2
  10.7 0.2 reduce-window.8
  10.9 0.1 convert_reduce_fusion.1
  11.0 0.1 convert_reduce_fusion
  11.1 0.3 fusion.18
  12.1 0.0 collective-permute-done
  12.1 0.0 copy-start.3
  12.1 3.4 %collective-permute-start.4 = (bf16[128,256]{1,0:T(8,128)(2,1)S(1)}, bf16[128,256]{1,0:T(8,128)(2,1)S(1)}, u32[]{:S(2)}, u32[]{:S(2)}) collective-permute-start(bf16[128,256]{1,0:T(8,128)(2,1)S(1)} %broadcast_select_fusion.3), channel_id=1, source_target_pairs={{0,4},{4,8},{8,12},{12,16},{16,20},{20,24},{24,28},{28,32},{32,36}... | collective-permute-start | bytes 196616 | tf_op jit(solution)/shard_map/ppermute | solution.py:28
  15.5 4.6 %collective-permute-start.3 = (bf16[128,256]{1,0:T(8,128)(2,1)S(1)}, bf16[128,256]{1,0:T(8,128)(2,1)S(1)}, u32[]{:S(2)}, u32[]{:S(2)}) collective-permute-start(bf16[128,256]{1,0:T(8,128)(2,1)S(1)} %broadcast_select_fusion.3), channel_id=1, source_target_pairs={{0,8},{4,12},{8,16},{12,20},{16,24},{20,28},{24,32},{28,36},{32,40... | collective-permute-start | bytes 196616 | tf_op jit(solution)/shard_map/ppermute | solution.py:28
  20.2 0.0 collective-permute-done.5
  20.2 3.8 %collective-permute-start.2 = (bf16[128,256]{1,0:T(8,128)(2,1)S(1)}, bf16[128,256]{1,0:T(8,128)(2,1)S(1)}, u32[]{:S(2)}, u32[]{:S(2)}) collective-permute-start(bf16[128,256]{1,0:T(8,128)(2,1)S(1)} %broadcast_select_fusion.3), channel_id=1, source_target_pairs={{0,12},{4,16},{8,20},{12,24},{16,28},{20,32},{24,36},{28,40},{32,4... | collective-permute-start | bytes 196616 | tf_op jit(solution)/shard_map/ppermute | solution.py:28
  24.0 0.0 collective-permute-done.11
  24.0 2.9 %collective-permute-start.1 = (bf16[128,256]{1,0:T(8,128)(2,1)S(1)}, bf16[128,256]{1,0:T(8,128)(2,1)S(1)}, u32[]{:S(2)}, u32[]{:S(2)}) collective-permute-start(bf16[128,256]{1,0:T(8,128)(2,1)S(1)} %broadcast_select_fusion.3), channel_id=1, source_target_pairs={{0,16},{4,20},{8,24},{12,28},{16,32},{20,36},{24,40},{28,44},{32,4... | collective-permute-start | bytes 196616 | tf_op jit(solution)/shard_map/ppermute | solution.py:28
  27.0 0.0 collective-permute-done.10
  27.0 2.9 %collective-permute-start.6 = (bf16[128,256]{1,0:T(8,128)(2,1)S(1)}, bf16[128,256]{1,0:T(8,128)(2,1)S(1)}, u32[]{:S(2)}, u32[]{:S(2)}) collective-permute-start(bf16[128,256]{1,0:T(8,128)(2,1)S(1)} %broadcast_select_fusion.2), channel_id=1, source_target_pairs={{0,16},{4,20},{8,24},{12,28},{16,32},{20,36},{24,40},{28,44},{32,4... | collective-permute-start | bytes 196616 | tf_op jit(solution)/shard_map/ppermute | solution.py:28
  30.0 4.4 %collective-permute-done.6 = bf16[128,256]{1,0:T(8,128)(2,1)S(1)} collective-permute-done((bf16[128,256]{1,0:T(8,128)(2,1)S(1)}, bf16[128,256]{1,0:T(8,128)(2,1)S(1)}, u32[]{:S(2)}, u32[]{:S(2)}) %collective-permute-start.6) | collective-permute-done | bytes 65568 | tf_op jit(solution)/shard_map/ppermute | solution.py:28
  34.3 2.3 %collective-permute-start.7 = (bf16[128,256]{1,0:T(8,128)(2,1)S(1)}, bf16[128,256]{1,0:T(8,128)(2,1)S(1)}, u32[]{:S(2)}, u32[]{:S(2)}) collective-permute-start(bf16[128,256]{1,0:T(8,128)(2,1)S(1)} %broadcast_select_fusion.2), channel_id=1, source_target_pairs={{0,12},{4,16},{8,20},{12,24},{16,28},{20,32},{24,36},{28,40},{32,4... | collective-permute-start | bytes 196616 | tf_op jit(solution)/shard_map/ppermute | solution.py:28
  36.6 6.0 %collective-permute-done.7 = bf16[128,256]{1,0:T(8,128)(2,1)S(1)} collective-permute-done((bf16[128,256]{1,0:T(8,128)(2,1)S(1)}, bf16[128,256]{1,0:T(8,128)(2,1)S(1)}, u32[]{:S(2)}, u32[]{:S(2)}) %collective-permute-start.7) | collective-permute-done | bytes 65568 | tf_op jit(solution)/shard_map/ppermute | solution.py:28
  42.6 2.9 %collective-permute-start.8 = (bf16[128,256]{1,0:T(8,128)(2,1)S(1)}, bf16[128,256]{1,0:T(8,128)(2,1)S(1)}, u32[]{:S(2)}, u32[]{:S(2)}) collective-permute-start(bf16[128,256]{1,0:T(8,128)(2,1)S(1)} %broadcast_select_fusion.2), channel_id=1, source_target_pairs={{0,8},{4,12},{8,16},{12,20},{16,24},{20,28},{24,32},{28,36},{32,40... | collective-permute-start | bytes 196616 | tf_op jit(solution)/shard_map/ppermute | solution.py:28
  45.5 6.9 %collective-permute-done.8 = bf16[128,256]{1,0:T(8,128)(2,1)S(1)} collective-permute-done((bf16[128,256]{1,0:T(8,128)(2,1)S(1)}, bf16[128,256]{1,0:T(8,128)(2,1)S(1)}, u32[]{:S(2)}, u32[]{:S(2)}) %collective-permute-start.8) | collective-permute-done | bytes 65568 | tf_op jit(solution)/shard_map/ppermute | solution.py:28
  52.4 2.5 %collective-permute-start.9 = (bf16[128,256]{1,0:T(8,128)(2,1)S(1)}, bf16[128,256]{1,0:T(8,128)(2,1)S(1)}, u32[]{:S(2)}, u32[]{:S(2)}) collective-permute-start(bf16[128,256]{1,0:T(8,128)(2,1)S(1)} %broadcast_select_fusion.2), channel_id=1, source_target_pairs={{0,4},{4,8},{8,12},{12,16},{16,20},{20,24},{24,28},{28,32},{32,36}... | collective-permute-start | bytes 196616 | tf_op jit(solution)/shard_map/ppermute | solution.py:28
  54.9 7.0 %collective-permute-done.9 = bf16[128,256]{1,0:T(8,128)(2,1)S(1)} collective-permute-done((bf16[128,256]{1,0:T(8,128)(2,1)S(1)}, bf16[128,256]{1,0:T(8,128)(2,1)S(1)}, u32[]{:S(2)}, u32[]{:S(2)}) %collective-permute-start.9) | collective-permute-done | bytes 65568 | tf_op jit(solution)/shard_map/ppermute | solution.py:28
  61.9 0.0 collective-permute-done.1
  62.0 0.4 fusion.51
  62.4 0.6 fusion.15
  63.0 0.7 convolution_bitcast_fusion.2
  63.7 0.3 multiply_reduce_fusion
  64.0 0.1 multiply_convert_fusion
  64.1 0.3 fusion.13
  64.4 0.2 fusion.10
  64.6 0.4 fusion.52
  65.0 0.6 fusion.14
  65.7 0.7 convolution_bitcast_fusion.3
  66.4 0.3 multiply_reduce_fusion.1
  66.7 0.1 multiply_convert_fusion.1
  66.8 0.3 fusion.12
  67.0 0.2 fusion.11
  67.3 0.1 copy.88
  67.5 0.1 copy.84
  67.6 0.7 pad_maximum_fusion.2
  68.3 4.9 %all-to-all-start = ((bf16[4,32,512]{2,1,0:T(8,128)(2,1)}), bf16[4,32,512]{2,1,0:T(8,128)(2,1)S(1)}, u32[]{:S(2)}, u32[]{:S(2)}) async-start(bf16[4,32,512]{2,1,0:T(8,128)(2,1)} %pad_maximum_fusion.2), calls=%async_computation | async-start | bytes 262144 | tf_op jit(solution)/shard_map/all_to_all | solution.py:122
  73.3 1.9 %collective-permute-start.12 = (f32[128,256]{0,1:T(8,128)S(1)}, f32[128,256]{0,1:T(8,128)S(1)}, u32[]{:S(2)}, u32[]{:S(2)}) collective-permute-start(f32[128,256]{0,1:T(8,128)S(1)} %get-tuple-element.24), channel_id=1, source_target_pairs={{4,0},{8,4},{12,8},{16,12},{20,16},{24,20},{28,24},{32,28},{36,32}... | collective-permute-start | bytes 393224 | tf_op jit(solution)/shard_map/ppermute | solution.py:28
  75.2 1.9 %collective-permute-start.13 = (f32[128,256]{0,1:T(8,128)S(1)}, f32[128,256]{0,1:T(8,128)S(1)}, u32[]{:S(2)}, u32[]{:S(2)}) collective-permute-start(f32[128,256]{0,1:T(8,128)S(1)} %get-tuple-element.25), channel_id=1, source_target_pairs={{8,0},{12,4},{16,8},{20,12},{24,16},{28,20},{32,24},{36,28},{40,32... | collective-permute-start | bytes 393224 | tf_op jit(solution)/shard_map/ppermute | solution.py:28
  77.1 1.9 %collective-permute-start.15 = (f32[128,256]{0,1:T(8,128)S(1)}, f32[128,256]{0,1:T(8,128)S(1)}, u32[]{:S(2)}, u32[]{:S(2)}) collective-permute-start(f32[128,256]{0,1:T(8,128)S(1)} %get-tuple-element.26), channel_id=1, source_target_pairs={{16,0},{20,4},{24,8},{28,12},{32,16},{36,20},{40,24},{44,28},{48,3... | collective-permute-start | bytes 393224 | tf_op jit(solution)/shard_map/ppermute | solution.py:28
  79.0 1.9 %collective-permute-start.14 = (f32[128,256]{0,1:T(8,128)S(1)}, f32[128,256]{0,1:T(8,128)S(1)}, u32[]{:S(2)}, u32[]{:S(2)}) collective-permute-start(f32[128,256]{0,1:T(8,128)S(1)} %get-tuple-element.27), channel_id=1, source_target_pairs={{12,0},{16,4},{20,8},{24,12},{28,16},{32,20},{36,24},{40,28},{44,3... | collective-permute-start | bytes 393224 | tf_op jit(solution)/shard_map/ppermute | solution.py:28
  81.0 0.1 copy.98
  81.1 0.1 copy.97
  81.2 4.5 %collective-permute-start.16 = (f32[128,256]{0,1:T(8,128)S(1)}, f32[128,256]{0,1:T(8,128)S(1)}, u32[]{:S(2)}, u32[]{:S(2)}) collective-permute-start(f32[128,256]{0,1:T(8,128)S(1)} %get-tuple-element.20), channel_id=1, source_target_pairs={{4,0},{8,4},{12,8},{16,12},{20,16},{24,20},{28,24},{32,28},{36,32}... | collective-permute-start | bytes 393224 | tf_op jit(solution)/shard_map/ppermute | solution.py:28
  85.8 0.7 maximum_bitcast_fusion
  86.4 0.1 copy.89
  86.5 0.7 broadcast_in_dim.26
  87.3 3.8 %collective-permute-start.17 = (f32[128,256]{0,1:T(8,128)S(1)}, f32[128,256]{0,1:T(8,128)S(1)}, u32[]{:S(2)}, u32[]{:S(2)}) collective-permute-start(f32[128,256]{0,1:T(8,128)S(1)} %get-tuple-element.21), channel_id=1, source_target_pairs={{8,0},{12,4},{16,8},{20,12},{24,16},{28,20},{32,24},{36,28},{40,32... | collective-permute-start | bytes 393224 | tf_op jit(solution)/shard_map/ppermute | solution.py:28
  91.1 7.7 %collective-permute-start.19 = (f32[128,256]{0,1:T(8,128)S(1)}, f32[128,256]{0,1:T(8,128)S(1)}, u32[]{:S(2)}, u32[]{:S(2)}) collective-permute-start(f32[128,256]{0,1:T(8,128)S(1)} %get-tuple-element.22), channel_id=1, source_target_pairs={{16,0},{20,4},{24,8},{28,12},{32,16},{36,20},{40,24},{44,28},{48,3... | collective-permute-start | bytes 393224 | tf_op jit(solution)/shard_map/ppermute | solution.py:28
  98.8 2.8 %collective-permute-start.18 = (f32[128,256]{0,1:T(8,128)S(1)}, f32[128,256]{0,1:T(8,128)S(1)}, u32[]{:S(2)}, u32[]{:S(2)}) collective-permute-start(f32[128,256]{0,1:T(8,128)S(1)} %get-tuple-element.23), channel_id=1, source_target_pairs={{12,0},{16,4},{20,8},{24,12},{28,16},{32,20},{36,24},{40,28},{44,3... | collective-permute-start | bytes 393224 | tf_op jit(solution)/shard_map/ppermute | solution.py:28
  101.6 0.7 copy.103
  102.3 4.5 %collective-permute-done.18 = f32[128,256]{0,1:T(8,128)S(1)} collective-permute-done((f32[128,256]{0,1:T(8,128)S(1)}, f32[128,256]{0,1:T(8,128)S(1)}, u32[]{:S(2)}, u32[]{:S(2)}) %collective-permute-start.18) | collective-permute-done | bytes 131104 | tf_op jit(solution)/shard_map/ppermute | solution.py:28
  106.9 0.7 copy.104
  (41 shorter events, 0.4 us)
Async XLA Ops:
  0.6 10.1 %copy-start = (s32[2,8]{1,0:T(2,128)S(1)}, s32[2,8]{1,0:T(2,128)}, u32[]{:S(2)}) copy-start(s32[2,8]{1,0:T(2,128)} %param.10) | copy-start | bytes 196
  0.6 11.4 %collective-permute-start = (bf16[128,256]{1,0:T(8,128)(2,1)}, bf16[128,256]{1,0:T(8,128)(2,1)S(1)}, u32[]{:S(2)}, u32[]{:S(2)}) collective-permute-start(bf16[128,256]{1,0:T(8,128)(2,1)} %bitcast.166), channel_id=1, source_target_pairs={{0,512},{512,0},{1,513},{513,1},{2,514},{514,2},{3,515},{515,3},{4... | collective-permute-start | bytes 196616 | tf_op jit(solution)/shard_map/ppermute | solution.py:22
  2.6 5.5 %copy-start.1 = (bf16[1,128,512]{2,1,0:T(8,128)(2,1)S(1)}, bf16[1,128,512]{2,1,0:T(8,128)(2,1)}, u32[]{:S(2)}) copy-start(bf16[1,128,512]{2,1,0:T(8,128)(2,1)} %param.6) | copy-start | bytes 393220
  2.6 17.6 %collective-permute-start.5 = (bf16[128,256]{1,0:T(8,128)(2,1)}, bf16[128,256]{1,0:T(8,128)(2,1)S(1)}, u32[]{:S(2)}, u32[]{:S(2)}) collective-permute-start(bf16[128,256]{1,0:T(8,128)(2,1)} %bitcast.167), channel_id=1, source_target_pairs={{0,512},{512,0},{1,513},{513,1},{2,514},{514,2},{3,515},{515,3},{4... | collective-permute-start | bytes 196616 | tf_op jit(solution)/shard_map/ppermute | solution.py:22
  6.2 17.9 %collective-permute-start.11 = (bf16[128,512]{0,1:T(8,128)(2,1)S(1)}, bf16[128,512]{0,1:T(8,128)(2,1)S(1)}, u32[]{:S(2)}, u32[]{:S(2)}) collective-permute-start(bf16[128,512]{0,1:T(8,128)(2,1)S(1)} %bitcast.154), channel_id=1, source_target_pairs={{0,512},{512,0},{1,513},{513,1},{2,514},{514,2},{3,515},{515,3},{4... | collective-permute-start | bytes 393224 | tf_op jit(solution)/shard_map/ppermute | solution.py:22
  8.2 18.7 %collective-permute-start.10 = (bf16[128,512]{0,1:T(8,128)(2,1)S(1)}, bf16[128,512]{0,1:T(8,128)(2,1)S(1)}, u32[]{:S(2)}, u32[]{:S(2)}) collective-permute-start(bf16[128,512]{0,1:T(8,128)(2,1)S(1)} %bitcast.155), channel_id=1, source_target_pairs={{0,512},{512,0},{1,513},{513,1},{2,514},{514,2},{3,515},{515,3},{4... | collective-permute-start | bytes 393224 | tf_op jit(solution)/shard_map/ppermute | solution.py:22
  10.7 1.4 %copy-start.2 = (bf16[1,128,256]{2,1,0:T(8,128)(2,1)S(1)}, bf16[1,128,256]{2,1,0:T(8,128)(2,1)}, u32[]{:S(2)}) copy-start(bf16[1,128,256]{2,1,0:T(8,128)(2,1)} %param.8) | copy-start | bytes 196612
  12.1 11.9 %copy-start.3 = (bf16[1,128,256]{2,1,0:T(8,128)(2,1)S(1)}, bf16[1,128,256]{2,1,0:T(8,128)(2,1)}, u32[]{:S(2)}) copy-start(bf16[1,128,256]{2,1,0:T(8,128)(2,1)} %param.7) | copy-start | bytes 196612
  12.1 49.8 %collective-permute-start.4 = (bf16[128,256]{1,0:T(8,128)(2,1)S(1)}, bf16[128,256]{1,0:T(8,128)(2,1)S(1)}, u32[]{:S(2)}, u32[]{:S(2)}) collective-permute-start(bf16[128,256]{1,0:T(8,128)(2,1)S(1)} %broadcast_select_fusion.3), channel_id=1, source_target_pairs={{0,4},{4,8},{8,12},{12,16},{16,20},{20,24},{24,28},{28,32},{32,36}... | collective-permute-start | bytes 196616 | tf_op jit(solution)/shard_map/ppermute | solution.py:28
  15.5 46.4 %collective-permute-start.3 = (bf16[128,256]{1,0:T(8,128)(2,1)S(1)}, bf16[128,256]{1,0:T(8,128)(2,1)S(1)}, u32[]{:S(2)}, u32[]{:S(2)}) collective-permute-start(bf16[128,256]{1,0:T(8,128)(2,1)S(1)} %broadcast_select_fusion.3), channel_id=1, source_target_pairs={{0,8},{4,12},{8,16},{12,20},{16,24},{20,28},{24,32},{28,36},{32,40... | collective-permute-start | bytes 196616 | tf_op jit(solution)/shard_map/ppermute | solution.py:28
  20.2 41.7 %collective-permute-start.2 = (bf16[128,256]{1,0:T(8,128)(2,1)S(1)}, bf16[128,256]{1,0:T(8,128)(2,1)S(1)}, u32[]{:S(2)}, u32[]{:S(2)}) collective-permute-start(bf16[128,256]{1,0:T(8,128)(2,1)S(1)} %broadcast_select_fusion.3), channel_id=1, source_target_pairs={{0,12},{4,16},{8,20},{12,24},{16,28},{20,32},{24,36},{28,40},{32,4... | collective-permute-start | bytes 196616 | tf_op jit(solution)/shard_map/ppermute | solution.py:28
  24.0 37.8 %collective-permute-start.1 = (bf16[128,256]{1,0:T(8,128)(2,1)S(1)}, bf16[128,256]{1,0:T(8,128)(2,1)S(1)}, u32[]{:S(2)}, u32[]{:S(2)}) collective-permute-start(bf16[128,256]{1,0:T(8,128)(2,1)S(1)} %broadcast_select_fusion.3), channel_id=1, source_target_pairs={{0,16},{4,20},{8,24},{12,28},{16,32},{20,36},{24,40},{28,44},{32,4... | collective-permute-start | bytes 196616 | tf_op jit(solution)/shard_map/ppermute | solution.py:28
  27.0 7.4 %collective-permute-start.6 = (bf16[128,256]{1,0:T(8,128)(2,1)S(1)}, bf16[128,256]{1,0:T(8,128)(2,1)S(1)}, u32[]{:S(2)}, u32[]{:S(2)}) collective-permute-start(bf16[128,256]{1,0:T(8,128)(2,1)S(1)} %broadcast_select_fusion.2), channel_id=1, source_target_pairs={{0,16},{4,20},{8,24},{12,28},{16,32},{20,36},{24,40},{28,44},{32,4... | collective-permute-start | bytes 196616 | tf_op jit(solution)/shard_map/ppermute | solution.py:28
  34.3 8.3 %collective-permute-start.7 = (bf16[128,256]{1,0:T(8,128)(2,1)S(1)}, bf16[128,256]{1,0:T(8,128)(2,1)S(1)}, u32[]{:S(2)}, u32[]{:S(2)}) collective-permute-start(bf16[128,256]{1,0:T(8,128)(2,1)S(1)} %broadcast_select_fusion.2), channel_id=1, source_target_pairs={{0,12},{4,16},{8,20},{12,24},{16,28},{20,32},{24,36},{28,40},{32,4... | collective-permute-start | bytes 196616 | tf_op jit(solution)/shard_map/ppermute | solution.py:28
  42.6 9.8 %collective-permute-start.8 = (bf16[128,256]{1,0:T(8,128)(2,1)S(1)}, bf16[128,256]{1,0:T(8,128)(2,1)S(1)}, u32[]{:S(2)}, u32[]{:S(2)}) collective-permute-start(bf16[128,256]{1,0:T(8,128)(2,1)S(1)} %broadcast_select_fusion.2), channel_id=1, source_target_pairs={{0,8},{4,12},{8,16},{12,20},{16,24},{20,28},{24,32},{28,36},{32,40... | collective-permute-start | bytes 196616 | tf_op jit(solution)/shard_map/ppermute | solution.py:28
  52.4 9.5 %collective-permute-start.9 = (bf16[128,256]{1,0:T(8,128)(2,1)S(1)}, bf16[128,256]{1,0:T(8,128)(2,1)S(1)}, u32[]{:S(2)}, u32[]{:S(2)}) collective-permute-start(bf16[128,256]{1,0:T(8,128)(2,1)S(1)} %broadcast_select_fusion.2), channel_id=1, source_target_pairs={{0,4},{4,8},{8,12},{12,16},{16,20},{20,24},{24,28},{28,32},{32,36}... | collective-permute-start | bytes 196616 | tf_op jit(solution)/shard_map/ppermute | solution.py:28
  68.3 18.1 %all-to-all-start = ((bf16[4,32,512]{2,1,0:T(8,128)(2,1)}), bf16[4,32,512]{2,1,0:T(8,128)(2,1)S(1)}, u32[]{:S(2)}, u32[]{:S(2)}) async-start(bf16[4,32,512]{2,1,0:T(8,128)(2,1)} %pad_maximum_fusion.2), calls=%async_computation | async-start | bytes 262144 | tf_op jit(solution)/shard_map/all_to_all | solution.py:122
  73.3 14.0 %collective-permute-start.12 = (f32[128,256]{0,1:T(8,128)S(1)}, f32[128,256]{0,1:T(8,128)S(1)}, u32[]{:S(2)}, u32[]{:S(2)}) collective-permute-start(f32[128,256]{0,1:T(8,128)S(1)} %get-tuple-element.24), channel_id=1, source_target_pairs={{4,0},{8,4},{12,8},{16,12},{20,16},{24,20},{28,24},{32,28},{36,32}... | collective-permute-start | bytes 393224 | tf_op jit(solution)/shard_map/ppermute | solution.py:28
  75.2 15.9 %collective-permute-start.13 = (f32[128,256]{0,1:T(8,128)S(1)}, f32[128,256]{0,1:T(8,128)S(1)}, u32[]{:S(2)}, u32[]{:S(2)}) collective-permute-start(f32[128,256]{0,1:T(8,128)S(1)} %get-tuple-element.25), channel_id=1, source_target_pairs={{8,0},{12,4},{16,8},{20,12},{24,16},{28,20},{32,24},{36,28},{40,32... | collective-permute-start | bytes 393224 | tf_op jit(solution)/shard_map/ppermute | solution.py:28
  77.1 21.6 %collective-permute-start.15 = (f32[128,256]{0,1:T(8,128)S(1)}, f32[128,256]{0,1:T(8,128)S(1)}, u32[]{:S(2)}, u32[]{:S(2)}) collective-permute-start(f32[128,256]{0,1:T(8,128)S(1)} %get-tuple-element.26), channel_id=1, source_target_pairs={{16,0},{20,4},{24,8},{28,12},{32,16},{36,20},{40,24},{44,28},{48,3... | collective-permute-start | bytes 393224 | tf_op jit(solution)/shard_map/ppermute | solution.py:28
  79.0 22.5 %collective-permute-start.14 = (f32[128,256]{0,1:T(8,128)S(1)}, f32[128,256]{0,1:T(8,128)S(1)}, u32[]{:S(2)}, u32[]{:S(2)}) collective-permute-start(f32[128,256]{0,1:T(8,128)S(1)} %get-tuple-element.27), channel_id=1, source_target_pairs={{12,0},{16,4},{20,8},{24,12},{28,16},{32,20},{36,24},{40,28},{44,3... | collective-permute-start | bytes 393224 | tf_op jit(solution)/shard_map/ppermute | solution.py:28
  81.2 21.1 %collective-permute-start.16 = (f32[128,256]{0,1:T(8,128)S(1)}, f32[128,256]{0,1:T(8,128)S(1)}, u32[]{:S(2)}, u32[]{:S(2)}) collective-permute-start(f32[128,256]{0,1:T(8,128)S(1)} %get-tuple-element.20), channel_id=1, source_target_pairs={{4,0},{8,4},{12,8},{16,12},{20,16},{24,20},{28,24},{32,28},{36,32}... | collective-permute-start | bytes 393224 | tf_op jit(solution)/shard_map/ppermute | solution.py:28
  87.3 15.1 %collective-permute-start.17 = (f32[128,256]{0,1:T(8,128)S(1)}, f32[128,256]{0,1:T(8,128)S(1)}, u32[]{:S(2)}, u32[]{:S(2)}) collective-permute-start(f32[128,256]{0,1:T(8,128)S(1)} %get-tuple-element.21), channel_id=1, source_target_pairs={{8,0},{12,4},{16,8},{20,12},{24,16},{28,20},{32,24},{36,28},{40,32... | collective-permute-start | bytes 393224 | tf_op jit(solution)/shard_map/ppermute | solution.py:28
  91.1 11.3 %collective-permute-start.19 = (f32[128,256]{0,1:T(8,128)S(1)}, f32[128,256]{0,1:T(8,128)S(1)}, u32[]{:S(2)}, u32[]{:S(2)}) collective-permute-start(f32[128,256]{0,1:T(8,128)S(1)} %get-tuple-element.22), channel_id=1, source_target_pairs={{16,0},{20,4},{24,8},{28,12},{32,16},{36,20},{40,24},{44,28},{48,3... | collective-permute-start | bytes 393224 | tf_op jit(solution)/shard_map/ppermute | solution.py:28
  98.8 8.1 %collective-permute-start.18 = (f32[128,256]{0,1:T(8,128)S(1)}, f32[128,256]{0,1:T(8,128)S(1)}, u32[]{:S(2)}, u32[]{:S(2)}) collective-permute-start(f32[128,256]{0,1:T(8,128)S(1)} %get-tuple-element.23), channel_id=1, source_target_pairs={{12,0},{16,4},{20,8},{24,12},{28,16},{32,20},{36,24},{40,28},{44,3... | collective-permute-start | bytes 393224 | tf_op jit(solution)/shard_map/ppermute | solution.py:28
where the time goes:
time: 108 us
  starting transfers between devices  65.4 us (61%)
  waiting for transfers between devices  28.7 us (27%)
  matrix products  5.04 us (5%)
  local copies, waits for them, and re-layouts  4.15 us (4%)
  other arithmetic  2.41 us (2%)
  between operations  1.92 us (2%)
    ppermute x16, starting transfers between devices, from_behind(): return lax.ppermute(block, axis, route)  51.7 us
    ppermute x16, waiting for transfers between devices, from_behind(): return lax.ppermute(block, axis, route)  28.7 us
    ppermute x4, starting transfers between devices, from_partner(): return lax.ppermute(block, axis, route)  8.79 us
    all_to_all x1, starting transfers between devices, body(): lax.all_to_all(attended, 'tp', split_axis=0, concat_axis=1, tiled=True)  4.9 us
    unnamed x20, local copies, waits for them, and re-layouts  2.71 us
  transfers between devices with their start and end apart: 21, of which 5 were waited for; matrix products, arithmetic and copies ran while one was open for 4% of the time, Pallas kernels for 0%

commit v1 on v0

v1 whole, which is shorter than its diff:
```python
import functools

import jax
import jax.numpy as jnp
from jax import lax
from jax.experimental import pallas as pl
from jax.experimental.pallas import tpu as pltpu
from jax.sharding import PartitionSpec as P

HD = 128
REP = 2
W = 512
BLK = 128
REACH = W // BLK
NX = 4
QW = REP * HD
QL = REP * BLK

SCALE = 168.0 ** (-0.5)
NEGATIVE = -1e30
MESH = pl.DeviceIdType.MESH
NT = (((1,), (1,)), ((), ()))
TN = (((0,), (0,)), ((), ()))
NN = (((1,), (0,)), ((), ()))


def mm(a, b, dims):
    return lax.dot_general(a, b, dims, preferred_element_type=jnp.float32)


def kernel(
    n_ctx, n_tp,
    q_ref, k_ref, v_ref, g_ref, len_ref, swap_ref,
    ao_ref, gq_ref, gk_ref, gv_ref,
    kb0, kb1, kb2, kb3, kb4, vb0, vb1, vb2, vb3, vb4, qb, gb, flags,
    ks, vs, qs, gs, sc, dp, pb, dsb,
    ob, dqb, part, own, mate, near, far, hub, relay,
    loc_sem, send_sem, rk_sem, rv_sem, rq_sem, rf_sem, out_sem, pd_sem, hub_sem,
):
    kb = (kb0, kb1, kb2, kb3, kb4)
    vb = (vb0, vb1, vb2, vb3, vb4)
    p = lax.axis_index("dp")
    c = lax.axis_index("ctx")
    y = lax.axis_index("tp")
    other = 1 - p
    x = lax.rem(c, NX)
    ahead = lax.rem(c + NX, n_ctx)
    behind = lax.rem(c + n_ctx - NX, n_ctx)

    barrier = pltpu.get_barrier_semaphore()
    partners = [(other, c, y)]
    for d in range(1, NX):
        for j in range(2):
            partners.append((j, c - x + lax.rem(x + d, NX), y))
    for j in range(2):
        partners.append((j, ahead, y))
        partners.append((j, behind, y))
    for d in range(1, n_tp):
        for j in range(2):
            partners.append((j, c, lax.rem(y + d, n_tp)))
    for dev in partners:
        pl.semaphore_signal(barrier, inc=1, device_id=dev, device_id_type=MESH)
    pl.semaphore_wait(barrier, len(partners))

    count = [0]
    waits = []

    def remote(src, dst, recv, dev, cond=None):
        sem = send_sem.at[count[0]]
        count[0] += 1
        cp = pltpu.make_async_remote_copy(
            src_ref=src, dst_ref=dst, send_sem=sem, recv_sem=recv,
            device_id=dev, device_id_type=MESH,
        )
        if cond is None:
            cp.start()
        else:
            @pl.when(cond)
            def _():
                cp.start()
        waits.append((cp, cond))
        return cp

    def arrived(ref, sem):
        pltpu.make_async_copy(ref, ref, sem).wait()

    def cols(ref, j, width):
        return ref.at[0, :, pl.ds(pl.multiple_of(j * width, width), width)]

    mine = (other, c, y)
    remote(cols(k_ref, other, HD), kb0.at[p], rk_sem.at[0], mine)
    remote(cols(q_ref, other, QW), qb.at[p], rq_sem.at[0], mine)
    for j in range(2):
        remote(cols(k_ref, j, HD), kb4.at[p], rk_sem.at[4], (j, ahead, y))
    remote(cols(v_ref, other, HD), vb0.at[p], rv_sem.at[0], mine)
    remote(cols(g_ref, other, QW), gb.at[p], rq_sem.at[1], mine)
    for j in range(2):
        remote(cols(v_ref, j, HD), vb4.at[p], rv_sem.at[4], (j, ahead, y))
    local = [
        pltpu.make_async_copy(cols(k_ref, p, HD), kb0.at[p], loc_sem.at[0]),
        pltpu.make_async_copy(cols(q_ref, p, QW), qb.at[p], loc_sem.at[1]),
        pltpu.make_async_copy(cols(v_ref, p, HD), vb0.at[p], loc_sem.at[2]),
        pltpu.make_async_copy(cols(g_ref, p, QW), gb.at[p], loc_sem.at[3]),
        pltpu.make_async_copy(swap_ref, flags.at[0], loc_sem.at[4]),
    ]
    for cp in local:
        cp.start()
    remote(swap_ref, flags.at[4], rf_sem.at[4], (p, ahead, y))
    for d in range(1, NX):
        remote(swap_ref, flags.at[d], rf_sem.at[d], (p, lax.rem(c + d, n_ctx), y), x + d < NX)
    for src, dst, sem in ((k_ref, kb, rk_sem), (v_ref, vb, rv_sem)):
        for d in (1, 3, 2):
            ok = x + d < NX
            for j in range(2):
                remote(cols(src, j, HD), dst[d].at[p], sem.at[d], (j, lax.rem(c + d, n_ctx), y), ok)

    lane = lax.broadcasted_iota(jnp.int32, (1, BLK), 1)
    pos = c * BLK + lane
    lows = []
    for pi in range(2):
        low = jnp.maximum(pos - (W - 1), 0)
        end = jnp.int32(0)
        for r in range(len_ref.shape[1]):
            end = end + len_ref[pi, r]
            low = jnp.maximum(low, jnp.where(pos >= end, end, 0))
        lows.append(jnp.concatenate([low] * REP, axis=1) - c * BLK)
    lane2 = jnp.concatenate([lane] * REP, axis=1)
    row_id = lax.broadcasted_iota(jnp.int32, (BLK, QL), 0)

    def pick(ref, swapped, pi):
        a, b = ref[pi], ref[1 - pi]
        return jnp.where(swapped, b, a)

    def take(d):
        swapped = flags[d, 0] == 1
        for pi in range(2):
            key = pick(kb[d], swapped, pi)
            ks[pi, d] = key
            s = mm(key, qs[pi], NT) * SCALE
            ok = row_id - d * BLK >= lows[pi]
            if d == 0:
                ok = ok & (row_id <= lane2)
            sc[pi, d] = jnp.where(ok, s, NEGATIVE)

    def take_v(d):
        swapped = flags[d, 0] == 1
        for pi in range(2):
            val = pick(vb[d], swapped, pi)
            vs[pi, d] = val
            dp[pi, d] = mm(val, gs[pi], NT)

    for cp in local:
        cp.wait()
    swapped = flags[0, 0] == 1
    arrived(qb.at[other], rq_sem.at[0])
    for pi in range(2):
        t = pick(qb, swapped, pi)
        for r in range(REP):
            qs[pi, r * BLK:(r + 1) * BLK] = t[:, r * HD:(r + 1) * HD]
    arrived(kb0.at[other], rk_sem.at[0])
    take(0)
    arrived(gb.at[other], rq_sem.at[1])
    for pi in range(2):
        t = pick(gb, swapped, pi)
        for r in range(REP):
            gs[pi, r * BLK:(r + 1) * BLK] = t[:, r * HD:(r + 1) * HD]
    arrived(vb0.at[other], rv_sem.at[0])
    take_v(0)

    for buf, dst, sem in ((kb, kb, rk_sem), (vb, vb, rv_sem)):
        arrived(buf[4], sem.at[4])
        for e in (1, 3, 2):
            ok = x >= e
            remote(buf[4], dst[4 - e], sem.at[4 - e], (p, lax.rem(c + n_ctx - e, n_ctx), y), ok)
    arrived(flags.at[4], rf_sem.at[4])
    for e in range(1, NX):
        remote(flags.at[4], flags.at[4 - e], rf_sem.at[4 - e], (p, lax.rem(c + n_ctx - e, n_ctx), y), x >= e)
    take(4)
    take_v(4)
    for d in (1, 2, 3):
        arrived(flags.at[d], rf_sem.at[d])
        arrived(kb[d], rk_sem.at[d])
        take(d)
    for d in (1, 2, 3):
        arrived(vb[d], rv_sem.at[d])
        take_v(d)

    for pi in range(2):
        top = jnp.max(sc[pi, 0], axis=0, keepdims=True)
        for d in range(1, REACH + 1):
            top = jnp.maximum(top, jnp.max(sc[pi, d], axis=0, keepdims=True))
        total = jnp.zeros((1, QL), jnp.float32)
        for d in range(REACH + 1):
            e = jnp.exp(sc[pi, d] - top)
            sc[pi, d] = e
            total = total + jnp.sum(e, axis=0, keepdims=True)
        inv = 1.0 / total
        delta = jnp.zeros((1, QL), jnp.float32)
        for d in range(REACH + 1):
            pr = sc[pi, d] * inv
            sc[pi, d] = pr
            pb[pi, d] = pr.astype(jnp.bfloat16)
            delta = delta + jnp.sum(pr * dp[pi, d], axis=0, keepdims=True)
        for d in range(REACH + 1):
            dsb[pi, d] = (sc[pi, d] * (dp[pi, d] - delta)).astype(jnp.bfloat16)

    def partial(d, dst):
        for pi in range(2):
            dk = mm(dsb[pi, d], qs[pi], NN) * SCALE
            dv = mm(pb[pi, d], gs[pi], NN)
            dst(pi, dk, dv)

    for d in (3, 2, 1):
        def put(pi, dk, dv, d=d):
            part[d, pi, 0] = dk.astype(jnp.bfloat16)
            part[d, pi, 1] = dv.astype(jnp.bfloat16)
        partial(d, put)
        dev = lax.rem(c + n_ctx - d, n_ctx)
        for pi in range(2):
            remote(part.at[d, pi], near.at[d - 1, p], pd_sem.at[d], (pi, dev, y), x >= d)
        remote(part.at[d], relay.at[NX - d - 1], hub_sem.at[NX - d], (p, c + NX - d, y), x < d)

    def put4(pi, dk, dv):
        hub[pi, 0] = dk
        hub[pi, 1] = dv
    partial(4, put4)

    def put0(pi, dk, dv):
        own[pi, 0] = dk
        own[pi, 1] = dv
    partial(0, put0)
    remote(own.at[other], mate, pd_sem.at[0], mine)

    for pi in range(2):
        o = mm(pb[pi].reshape(-1, QL), vs[pi].reshape(-1, HD), TN).astype(jnp.bfloat16)
        for r in range(REP):
            ob[pi, :, r * HD:(r + 1) * HD] = o[r * BLK:(r + 1) * BLK]
    share = BLK // n_tp
    width = REP * HD
    at = pl.ds(pl.multiple_of((y * 2 + p) * width, width), width)
    for dt in range(n_tp):
        t = lax.rem(y + dt, n_tp)
        rows = pl.ds(pl.multiple_of(t * share, share), share)
        for dj in range(2):
            pi = p if dj == 0 else other
            if dt == 0 and dj == 0:
                keep = pltpu.make_async_copy(ob.at[pi, rows], ao_ref.at[0, :, at], loc_sem.at[5])
                keep.start()
            else:
                remote(ob.at[pi, rows], ao_ref.at[0, :, at], out_sem.at[0], (pi, c, t))
    for pi in range(2):
        o = (mm(dsb[pi].reshape(-1, QL), ks[pi].reshape(-1, HD), TN) * SCALE).astype(jnp.bfloat16)
        for r in range(REP):
            dqb[pi, :, r * HD:(r + 1) * HD] = o[r * BLK:(r + 1) * BLK]
    keep_q = pltpu.make_async_copy(dqb.at[p], cols(gq_ref, p, QW), loc_sem.at[6])
    keep_q.start()
    remote(dqb.at[other], cols(gq_ref, p, QW), out_sem.at[1], mine)

    for e in range(1, NX):
        @pl.when(x >= e)
        def _():
            arrived(relay.at[e - 1], hub_sem.at[e])
            for pi in range(2):
                for s in range(2):
                    hub[pi, s] = hub[pi, s] + relay[e - 1, pi, s].astype(jnp.float32)
    for pi in range(2):
        for s in range(2):
            part[4, pi, s] = hub[pi, s].astype(jnp.bfloat16)
    for pi in range(2):
        remote(part.at[4, pi], far.at[p], pd_sem.at[4], (pi, behind, y))

    arrived(mate, pd_sem.at[0])
    for d in range(1, NX):
        @pl.when(x + d < NX)
        def _():
            arrived(near.at[d - 1], pd_sem.at[d])
            for s in range(2):
                own[p, s] = own[p, s] + near[d - 1, p, s].astype(jnp.float32)
                mate[s] = mate[s] + near[d - 1, other, s].astype(jnp.float32)
    arrived(far, pd_sem.at[4])
    for s, out in ((0, gk_ref), (1, gv_ref)):
        for j, src in ((p, own[p, s]), (other, mate[s])):
            out[0, :, pl.ds(pl.multiple_of(j * HD, HD), HD)] = (
                src + far[j, s].astype(jnp.float32)
            ).astype(jnp.bfloat16)

    keep.wait()
    keep_q.wait()
    arrived(ao_ref.at[0, :, pl.ds(0, (2 * n_tp - 1) * width)], out_sem.at[0])
    arrived(cols(gq_ref, other, QW), out_sem.at[1])
    for cp, cond in waits:
        if cond is None:
            cp.wait_send()
        else:
            @pl.when(cond)
            def _():
                cp.wait_send()


def body(n_ctx, n_tp, queries, key_rows, values, grad_out, lengths, pair_swap):
    bf, f32 = jnp.bfloat16, jnp.float32
    nd = REACH + 1
    kv_piece = pltpu.VMEM((2, BLK, HD), bf)
    any_spec = pl.BlockSpec(memory_space=pl.ANY)
    vmem_spec = pl.BlockSpec(memory_space=pltpu.VMEM)
    dma = pltpu.SemaphoreType.DMA
    return pl.pallas_call(
        functools.partial(kernel, n_ctx, n_tp),
        out_shape=(
            jax.ShapeDtypeStruct((1, BLK // n_tp, n_tp * 2 * QW), bf),
            jax.ShapeDtypeStruct(queries.shape, bf),
            jax.ShapeDtypeStruct(key_rows.shape, bf),
            jax.ShapeDtypeStruct(values.shape, bf),
        ),
        in_specs=[any_spec] * 4 + [pl.BlockSpec(memory_space=pltpu.SMEM), any_spec],
        out_specs=(any_spec, any_spec, vmem_spec, vmem_spec),
        scratch_shapes=[kv_piece] * 10 + [
            pltpu.VMEM((2, BLK, QW), bf),
            pltpu.VMEM((2, BLK, QW), bf),
            pltpu.SMEM((nd, 1), jnp.int32),
            pltpu.VMEM((2, nd, BLK, HD), bf),
            pltpu.VMEM((2, nd, BLK, HD), bf),
            pltpu.VMEM((2, QL, HD), bf),
            pltpu.VMEM((2, QL, HD), bf),
            pltpu.VMEM((2, nd, BLK, QL), f32),
            pltpu.VMEM((2, nd, BLK, QL), f32),
            pltpu.VMEM((2, nd, BLK, QL), bf),
            pltpu.VMEM((2, nd, BLK, QL), bf),
            pltpu.VMEM((2, BLK, QW), bf),
            pltpu.VMEM((2, BLK, QW), bf),
            pltpu.VMEM((nd, 2, 2, BLK, HD), bf),
            pltpu.VMEM((2, 2, BLK, HD), f32),
            pltpu.VMEM((2, BLK, HD), f32),
            pltpu.VMEM((3, 2, 2, BLK, HD), bf),
            pltpu.VMEM((2, 2, BLK, HD), bf),
            pltpu.VMEM((2, 2, BLK, HD), f32),
            pltpu.VMEM((3, 2, 2, BLK, HD), bf),
            dma((7,)),
            dma((64,)),
            dma((nd,)),
            dma((nd,)),
            dma((2,)),
            dma((nd,)),
            dma((2,)),
            dma((nd,)),
            dma((NX,)),
        ],
        compiler_params=pltpu.CompilerParams(collective_id=0, has_side_effects=True),
        name="attend",
    )(queries, key_rows, values, grad_out, lengths, pair_swap)


def solution(mesh):
    placed = P("dp", "ctx", "tp")
    return jax.shard_map(
        functools.partial(body, mesh.shape["ctx"], mesh.shape["tp"]),
        mesh=mesh,
        in_specs=(placed, placed, placed, placed, P(), P("ctx")),
        out_specs=(P("dp", ("ctx", "tp"), None), placed, placed, placed),
        check_vma=False,
    )
```

time: 108 us -> 53.4 us (0.49)
  the two profiles are of different devices: /device:TPU:648 before, /device:TPU:6 now
where the time goes in v1:
time: 53.4 us; the launch traced here: 53.1 us
  Pallas kernels  47.9 us (90%)
  local copies, waits for them, and re-layouts  3.96 us (7%)
  between operations  1.3 us (2%)
    pallas_call x1, Pallas kernels, body(): pl.pallas_call(functools.partial(kernel, n_ctx, n_tp), out_shape=(jax.Sha...  47.9 us
    unnamed x10, local copies, waits for them, and re-layouts  3.96 us

profile of v1, /device:TPU:6, one launch (start us, length us, event | category | flops | bytes accessed | tf_op | source)
XLA Modules:
  0.0 53.1 jit_solution(17816793543873398478)
XLA Ops:
  1.3 47.9 %attend.1 = (bf16[1,32,2048]{2,1,0:T(8,128)(2,1)}, bf16[1,128,512]{2,1,0:T(8,128)(2,1)}, bf16[1,128,256]{2,1,0:T(8,128)(2,1)}, bf16[1,128,256]{2,1,0:T(8,128)(2,1)}) custom-call(bf16[1,128,512]{2,1,0:T(8,128)(2,1)} %q_ref.1, bf16[1,128,256]{2,1,0:T(8,128)(2,1)} %k_ref.1, bf16[1,128,256]{2,1,0:T(8,128)(2,1)} %v_ref.1, bf16[1,128,512]{2,1,0:T(8,128)(2,1)} %g_ref.1, ...), custom_call_target="tpu_custom_call" | custom-call | tf_op jit(solution)/shard_map/attend/pallas_call | solution.py:307
  49.1 0.0 copy-start
  49.2 1.6 %copy.15 = bf16[1,32,2048]{2,1,0:T(8,128)(2,1)} copy(bf16[1,32,2048]{2,1,0:T(8,128)(2,1)} %get-tuple-element.8) | data formatting | bytes 262144
  50.8 0.0 copy-done
  50.8 0.0 copy-start.2
  50.8 0.7 %copy.16 = bf16[1,128,512]{2,1,0:T(8,128)(2,1)} copy(bf16[1,128,512]{2,1,0:T(8,128)(2,1)S(1)} %copy-done) | data formatting | bytes 262144
  51.4 0.2 copy-done.2
  51.6 0.0 copy-start.1
  51.6 0.6 %copy.17 = bf16[1,128,256]{2,1,0:T(8,128)(2,1)} copy(bf16[1,128,256]{2,1,0:T(8,128)(2,1)S(1)} %copy-done.2) | data formatting | bytes 131072
  52.3 0.2 copy-done.1
  52.5 0.6 %copy.18 = bf16[1,128,256]{2,1,0:T(8,128)(2,1)} copy(bf16[1,128,256]{2,1,0:T(8,128)(2,1)S(1)} %copy-done.1) | data formatting | bytes 131072
Async XLA Ops:
  49.1 1.6 %copy-start = (bf16[1,128,512]{2,1,0:T(8,128)(2,1)S(1)}, bf16[1,128,512]{2,1,0:T(8,128)(2,1)}, u32[]{:S(2)}) copy-start(bf16[1,128,512]{2,1,0:T(8,128)(2,1)} %get-tuple-element.9) | copy-start | bytes 393220
  50.8 0.9 %copy-start.2 = (bf16[1,128,256]{2,1,0:T(8,128)(2,1)S(1)}, bf16[1,128,256]{2,1,0:T(8,128)(2,1)}, u32[]{:S(2)}) copy-start(bf16[1,128,256]{2,1,0:T(8,128)(2,1)} %get-tuple-element.10) | copy-start | bytes 196612
  51.6 0.9 %copy-start.1 = (bf16[1,128,256]{2,1,0:T(8,128)(2,1)S(1)}, bf16[1,128,256]{2,1,0:T(8,128)(2,1)}, u32[]{:S(2)}) copy-start(bf16[1,128,256]{2,1,0:T(8,128)(2,1)} %get-tuple-element.11) | copy-start | bytes 196612

commit v2 on v1

v2 whole, which is shorter than its diff:
```python
import functools

import jax
import jax.numpy as jnp
from jax import lax
from jax.experimental import pallas as pl
from jax.experimental.pallas import tpu as pltpu
from jax.sharding import PartitionSpec as P

HD = 128
REP = 2
W = 512
BLK = 128
REACH = W // BLK
NX = 4
QW = REP * HD
QL = REP * BLK

SCALE = 168.0 ** (-0.5)
NEGATIVE = -1e30
MESH = pl.DeviceIdType.MESH
NT = (((1,), (1,)), ((), ()))
TN = (((0,), (0,)), ((), ()))
NN = (((1,), (0,)), ((), ()))


def mm(a, b, dims):
    return lax.dot_general(a, b, dims, preferred_element_type=jnp.float32)


def kernel(
    n_ctx, n_tp,
    q_ref, k_ref, v_ref, g_ref, len_ref, swap_ref,
    ao_ref, gq_ref, gk_ref, gv_ref,
    kb0, kb1, kb2, kb3, kb4, vb0, vb1, vb2, vb3, vb4, qb, gb, flags,
    ks, vs, qs, gs, sc, dp, pb, dsb,
    ob, dqb, part, own, mate, near, far, hub, relay,
    loc_sem, send_sem, rk_sem, rv_sem, rq_sem, rf_sem, out_sem, pd_sem, hub_sem,
):
    kb = (kb0, kb1, kb2, kb3, kb4)
    vb = (vb0, vb1, vb2, vb3, vb4)
    p = lax.axis_index("dp")
    c = lax.axis_index("ctx")
    y = lax.axis_index("tp")
    other = 1 - p
    x = lax.rem(c, NX)
    ahead = lax.rem(c + NX, n_ctx)
    behind = lax.rem(c + n_ctx - NX, n_ctx)

    first = c < NX
    final = c + NX >= n_ctx

    def cols(ref, j, width):
        return ref.at[0, :, pl.ds(pl.multiple_of(j * width, width), width)]

    local = [
        pltpu.make_async_copy(cols(k_ref, p, HD), kb0.at[p], loc_sem.at[0]),
        pltpu.make_async_copy(cols(q_ref, p, QW), qb.at[p], loc_sem.at[1]),
        pltpu.make_async_copy(cols(v_ref, p, HD), vb0.at[p], loc_sem.at[2]),
        pltpu.make_async_copy(cols(g_ref, p, QW), gb.at[p], loc_sem.at[3]),
    ]
    for cp in local:
        cp.start()

    barrier = pltpu.get_barrier_semaphore()

    def greet(dev):
        pl.semaphore_signal(barrier, inc=1, device_id=dev, device_id_type=MESH)

    greet((other, c, y))
    met = 1
    for d in range(1, NX):
        for j in range(2):
            greet((j, c - x + lax.rem(x + d, NX), y))
            met += 1
    for d in range(1, n_tp):
        for j in range(2):
            greet((j, c, lax.rem(y + d, n_tp)))
            met += 1

    @pl.when(jnp.logical_not(final))
    def _():
        for j in range(2):
            greet((j, ahead, y))

    @pl.when(jnp.logical_not(first))
    def _():
        for j in range(2):
            greet((j, behind, y))

    pl.semaphore_wait(barrier, met + 2 * (1 - first.astype(jnp.int32)) + 2 * (1 - final.astype(jnp.int32)))

    count = [0]
    waits = []

    def remote(src, dst, recv, dev, cond=None):
        sem = send_sem.at[count[0]]
        count[0] += 1
        cp = pltpu.make_async_remote_copy(
            src_ref=src, dst_ref=dst, send_sem=sem, recv_sem=recv,
            device_id=dev, device_id_type=MESH,
        )
        if cond is None:
            cp.start()
        else:
            @pl.when(cond)
            def _():
                cp.start()
        waits.append((cp, cond))
        return cp

    def arrived(ref, sem, cond=None):
        if cond is None:
            pltpu.make_async_copy(ref, ref, sem).wait()
        else:
            @pl.when(cond)
            def _():
                pltpu.make_async_copy(ref, ref, sem).wait()

    mine = (other, c, y)
    inner = jnp.logical_not(first)
    onward = jnp.logical_not(final)
    for j in range(2):
        remote(cols(k_ref, j, HD), kb4.at[p], rk_sem.at[4], (j, ahead, y), onward)
    remote(cols(k_ref, other, HD), kb0.at[p], rk_sem.at[0], mine)
    remote(cols(q_ref, other, QW), qb.at[p], rq_sem.at[0], mine)
    for d in (2, 1, 3):
        for j in range(2):
            remote(cols(k_ref, j, HD), kb[d].at[p], rk_sem.at[d], (j, lax.rem(c + d, n_ctx), y), x + d < NX)
    remote(cols(g_ref, other, QW), gb.at[p], rq_sem.at[1], mine)
    for j in range(2):
        remote(cols(v_ref, j, HD), vb4.at[p], rv_sem.at[4], (j, ahead, y), onward)
    remote(cols(v_ref, other, HD), vb0.at[p], rv_sem.at[0], mine)
    for d in (2, 1, 3):
        for j in range(2):
            remote(cols(v_ref, j, HD), vb[d].at[p], rv_sem.at[d], (j, lax.rem(c + d, n_ctx), y), x + d < NX)
    remote(swap_ref.at[0], flags.at[4], rf_sem.at[4], (p, ahead, y), onward)
    for d in range(1, NX):
        remote(swap_ref.at[0], flags.at[d], rf_sem.at[d], (p, lax.rem(c + d, n_ctx), y), x + d < NX)

    for d in range(1, REACH + 1):
        @pl.when(c < d)
        def _():
            flags[d, 0] = 0
            kb[d][...] = jnp.zeros_like(kb[d])
            vb[d][...] = jnp.zeros_like(vb[d])

    lane = lax.broadcasted_iota(jnp.int32, (1, BLK), 1)
    pos = c * BLK + lane
    lows = []
    for pi in range(2):
        low = jnp.maximum(pos - (W - 1), 0)
        end = jnp.int32(0)
        for r in range(len_ref.shape[1]):
            end = end + len_ref[pi, r]
            low = jnp.maximum(low, jnp.where(pos >= end, end, 0))
        lows.append(jnp.concatenate([low] * REP, axis=1) - c * BLK)
    lane2 = jnp.concatenate([lane] * REP, axis=1)
    row_id = lax.broadcasted_iota(jnp.int32, (BLK, QL), 0)

    def pick(ref, swapped, pi):
        a, b = ref[pi], ref[1 - pi]
        return jnp.where(swapped, b, a)

    def take(d):
        swapped = (swap_ref[0, 0] if d == 0 else flags[d, 0]) == 1
        for pi in range(2):
            key = pick(kb[d], swapped, pi)
            ks[pi, d] = key
            s = mm(key, qs[pi], NT) * SCALE
            ok = row_id - d * BLK >= lows[pi]
            if d == 0:
                ok = ok & (row_id <= lane2)
            sc[pi, d] = jnp.where(ok, s, NEGATIVE)

    def take_v(d):
        swapped = (swap_ref[0, 0] if d == 0 else flags[d, 0]) == 1
        for pi in range(2):
            val = pick(vb[d], swapped, pi)
            vs[pi, d] = val
            dp[pi, d] = mm(val, gs[pi], NT)

    def stack(src, dst, swapped):
        for pi in range(2):
            t = pick(src, swapped, pi)
            for r in range(REP):
                dst[pi, r * BLK:(r + 1) * BLK] = t[:, r * HD:(r + 1) * HD]

    for cp in local:
        cp.wait()
    swapped = swap_ref[0, 0] == 1
    arrived(qb.at[other], rq_sem.at[0])
    stack(qb, qs, swapped)
    arrived(kb0.at[other], rk_sem.at[0])
    take(0)
    arrived(gb.at[other], rq_sem.at[1])
    stack(gb, gs, swapped)

    def pass_on(buf, sem):
        arrived(buf[4], sem.at[4], inner)
        for e in (2, 1, 3):
            remote(buf[4], buf[4 - e], sem.at[4 - e], (p, lax.rem(c + n_ctx - e, n_ctx), y), inner & (x >= e))

    pass_on(kb, rk_sem)
    arrived(flags.at[4], rf_sem.at[4], inner)
    for e in range(1, NX):
        remote(flags.at[4], flags.at[4 - e], rf_sem.at[4 - e], (p, lax.rem(c + n_ctx - e, n_ctx), y), inner & (x >= e))
    take(4)
    pass_on(vb, rv_sem)
    arrived(vb0.at[other], rv_sem.at[0])
    take_v(0)
    take_v(4)
    for d in (1, 2, 3):
        arrived(flags.at[d], rf_sem.at[d], c >= d)
        arrived(kb[d], rk_sem.at[d], c >= d)
        take(d)

    def give(s, d):
        dev = lax.rem(c + n_ctx - d, n_ctx)
        for pi in range(2):
            remote(part.at[d, s, pi], near.at[d - 1, s, p], pd_sem.at[s, d], (pi, dev, y), x >= d)
        remote(part.at[d, s], relay.at[NX - d - 1, s], hub_sem.at[s, NX - d], (p, c + NX - d, y), inner & (x < d))

    for pi in range(2):
        top = jnp.max(sc[pi, 0], axis=0, keepdims=True)
        for d in range(1, REACH + 1):
            top = jnp.maximum(top, jnp.max(sc[pi, d], axis=0, keepdims=True))
        total = jnp.zeros((1, QL), jnp.float32)
        for d in range(REACH + 1):
            e = jnp.exp(sc[pi, d] - top)
            sc[pi, d] = e
            total = total + jnp.sum(e, axis=0, keepdims=True)
        inv = 1.0 / total
        for d in (3, 2, 1, 4, 0):
            pr = sc[pi, d] * inv
            sc[pi, d] = pr
            pb[pi, d] = pr.astype(jnp.bfloat16)
            dv = mm(pb[pi, d], gs[pi], NN)
            if d == 0:
                own[1, pi] = dv
            elif d == 4:
                hub[1, pi] = dv
            else:
                part[d, 1, pi] = dv.astype(jnp.bfloat16)
    for d in (3, 2, 1):
        give(1, d)
    remote(own.at[1, other], mate.at[1], pd_sem.at[1, 0], mine)

    for d in (1, 2, 3):
        arrived(vb[d], rv_sem.at[d], c >= d)
        take_v(d)
    for pi in range(2):
        delta = jnp.zeros((1, QL), jnp.float32)
        for d in range(REACH + 1):
            delta = delta + jnp.sum(sc[pi, d] * dp[pi, d], axis=0, keepdims=True)
        for d in (3, 2, 1, 4, 0):
            dsb[pi, d] = (sc[pi, d] * (dp[pi, d] - delta)).astype(jnp.bfloat16)
            dk = mm(dsb[pi, d], qs[pi], NN) * SCALE
            if d == 0:
                own[0, pi] = dk
            elif d == 4:
                hub[0, pi] = dk
            else:
                part[d, 0, pi] = dk.astype(jnp.bfloat16)
    for d in (3, 2, 1):
        give(0, d)
    remote(own.at[0, other], mate.at[0], pd_sem.at[0, 0], mine)

    for pi in range(2):
        o = mm(pb[pi].reshape(-1, QL), vs[pi].reshape(-1, HD), TN).astype(jnp.bfloat16)
        for r in range(REP):
            ob[pi, :, r * HD:(r + 1) * HD] = o[r * BLK:(r + 1) * BLK]
    share = BLK // n_tp
    width = REP * HD
    at = pl.ds(pl.multiple_of((y * 2 + p) * width, width), width)
    for dt in range(n_tp):
        t = lax.rem(y + dt, n_tp)
        rows = pl.ds(pl.multiple_of(t * share, share), share)
        for dj in range(2):
            pi = p if dj == 0 else other
            if dt == 0 and dj == 0:
                keep = pltpu.make_async_copy(ob.at[pi, rows], ao_ref.at[0, :, at], loc_sem.at[5])
                keep.start()
            else:
                remote(ob.at[pi, rows], ao_ref.at[0, :, at], out_sem.at[0], (pi, c, t))
    for pi in range(2):
        o = (mm(dsb[pi].reshape(-1, QL), ks[pi].reshape(-1, HD), TN) * SCALE).astype(jnp.bfloat16)
        for r in range(REP):
            dqb[pi, :, r * HD:(r + 1) * HD] = o[r * BLK:(r + 1) * BLK]
    keep_q = pltpu.make_async_copy(dqb.at[p], cols(gq_ref, p, QW), loc_sem.at[6])
    keep_q.start()
    remote(dqb.at[other], cols(gq_ref, p, QW), out_sem.at[1], mine)

    for s in (1, 0):
        for e in range(1, NX):
            @pl.when(inner & (x >= e))
            def _():
                arrived(relay.at[e - 1, s], hub_sem.at[s, e])
                for pi in range(2):
                    hub[s, pi] = hub[s, pi] + relay[e - 1, s, pi].astype(jnp.float32)
        for pi in range(2):
            part[4, s, pi] = hub[s, pi].astype(jnp.bfloat16)
        for pi in range(2):
            remote(part.at[4, s, pi], far.at[s, p], pd_sem.at[s, 4], (pi, behind, y), inner)

    for s, out in ((1, gv_ref), (0, gk_ref)):
        arrived(mate.at[s], pd_sem.at[s, 0])
        for d in range(1, NX):
            @pl.when(x + d < NX)
            def _():
                arrived(near.at[d - 1, s], pd_sem.at[s, d])
                own[s, p] = own[s, p] + near[d - 1, s, p].astype(jnp.float32)
                mate[s] = mate[s] + near[d - 1, s, other].astype(jnp.float32)

        @pl.when(onward)
        def _():
            arrived(far.at[s], pd_sem.at[s, 4])
            own[s, p] = own[s, p] + far[s, p].astype(jnp.float32)
            mate[s] = mate[s] + far[s, other].astype(jnp.float32)
        for j, src in ((p, own[s, p]), (other, mate[s])):
            out[0, :, pl.ds(pl.multiple_of(j * HD, HD), HD)] = src.astype(jnp.bfloat16)

    keep.wait()
    keep_q.wait()
    arrived(ao_ref.at[0, :, pl.ds(0, (2 * n_tp - 1) * width)], out_sem.at[0])
    arrived(cols(gq_ref, other, QW), out_sem.at[1])
    for cp, cond in waits:
        if cond is None:
            cp.wait_send()
        else:
            @pl.when(cond)
            def _():
                cp.wait_send()


def store(a_ref, b_ref, c_ref, d_ref, ao_ref, gq_ref, gk_ref, gv_ref, sem):
    copies = [
        pltpu.make_async_copy(src, dst, sem.at[i])
        for i, (src, dst) in enumerate(((a_ref, ao_ref), (b_ref, gq_ref), (c_ref, gk_ref), (d_ref, gv_ref)))
    ]
    for cp in copies:
        cp.start()
    for cp in copies:
        cp.wait()


def body(n_ctx, n_tp, queries, key_rows, values, grad_out, lengths, pair_swap):
    bf, f32 = jnp.bfloat16, jnp.float32
    nd = REACH + 1
    kv_piece = pltpu.VMEM((2, BLK, HD), bf)
    any_spec = pl.BlockSpec(memory_space=pl.ANY)
    vmem_spec = pl.BlockSpec(memory_space=pltpu.VMEM)
    dma = pltpu.SemaphoreType.DMA
    shapes = (
        ((1, BLK // n_tp, n_tp * 2 * QW), bf),
        (queries.shape, bf),
        (key_rows.shape, bf),
        (values.shape, bf),
    )
    held = pl.pallas_call(
        functools.partial(kernel, n_ctx, n_tp),
        out_shape=tuple(pltpu.VMEM(*item) for item in shapes),
        in_specs=[any_spec] * 4 + [pl.BlockSpec(memory_space=pltpu.SMEM)] * 2,
        out_specs=(vmem_spec,) * 4,
        scratch_shapes=[kv_piece] * 10 + [
            pltpu.VMEM((2, BLK, QW), bf),
            pltpu.VMEM((2, BLK, QW), bf),
            pltpu.SMEM((nd, 1), jnp.int32),
            pltpu.VMEM((2, nd, BLK, HD), bf),
            pltpu.VMEM((2, nd, BLK, HD), bf),
            pltpu.VMEM((2, QL, HD), bf),
            pltpu.VMEM((2, QL, HD), bf),
            pltpu.VMEM((2, nd, BLK, QL), f32),
            pltpu.VMEM((2, nd, BLK, QL), f32),
            pltpu.VMEM((2, nd, BLK, QL), bf),
            pltpu.VMEM((2, nd, BLK, QL), bf),
            pltpu.VMEM((2, BLK, QW), bf),
            pltpu.VMEM((2, BLK, QW), bf),
            pltpu.VMEM((nd, 2, 2, BLK, HD), bf),
            pltpu.VMEM((2, 2, BLK, HD), f32),
            pltpu.VMEM((2, BLK, HD), f32),
            pltpu.VMEM((3, 2, 2, BLK, HD), bf),
            pltpu.VMEM((2, 2, BLK, HD), bf),
            pltpu.VMEM((2, 2, BLK, HD), f32),
            pltpu.VMEM((3, 2, 2, BLK, HD), bf),
            dma((7,)),
            dma((80,)),
            dma((nd,)),
            dma((nd,)),
            dma((2,)),
            dma((nd,)),
            dma((2,)),
            dma((2, nd)),
            dma((2, NX)),
        ],
        compiler_params=pltpu.CompilerParams(collective_id=0, has_side_effects=True),
        name="attend",
    )(queries, key_rows, values, grad_out, lengths, pair_swap.reshape(1, 1))
    return pl.pallas_call(
        store,
        out_shape=tuple(jax.ShapeDtypeStruct(*item) for item in shapes),
        in_specs=[any_spec] * 4,
        out_specs=(any_spec,) * 4,
        scratch_shapes=[dma((4,))],
        name="store",
    )(*[pltpu.with_memory_space_constraint(item, pltpu.VMEM) for item in held])


def solution(mesh):
    placed = P("dp", "ctx", "tp")
    return jax.shard_map(
        functools.partial(body, mesh.shape["ctx"], mesh.shape["tp"]),
        mesh=mesh,
        in_specs=(placed, placed, placed, placed, P(), P("ctx")),
        out_specs=(P("dp", ("ctx", "tp"), None), placed, placed, placed),
        check_vma=False,
    )
```

time: 53.4 us -> 41.8 us (0.78)
  the two profiles are of different devices: /device:TPU:6 before, /device:TPU:5 now
where the time goes in v2:
time: 41.8 us; the launch traced here: 41.6 us
  Pallas kernels  40.3 us (96%)
  between operations  1.29 us (3%)
    pallas_call x1, Pallas kernels, body(): pl.pallas_call(functools.partial(kernel, n_ctx, n_tp), out_shape=tuple((p...  39.5 us

profile of v2, /device:TPU:5, one launch (start us, length us, event | category | flops | bytes accessed | tf_op | source)
XLA Modules:
  0.0 41.6 jit_solution(7286925359302279882)
XLA Ops:
  1.3 39.5 %attend.1 = (bf16[1,32,2048]{2,1,0:T(8,128)(2,1)S(1)}, bf16[1,128,512]{2,1,0:T(8,128)(2,1)S(1)}, bf16[1,128,256]{2,1,0:T(8,128)(2,1)S(1)}, bf16[1,128,256]{2,1,0:T(8,128)(2,1)S(1)}) custom-call(bf16[1,128,512]{2,1,0:T(8,128)(2,1)} %q_ref.1, bf16[1,128,256]{2,1,0:T(8,128)(2,1)} %k_ref.1, bf16[1,128,256]{2,1,0:T(8,128)(2,1)} %v_ref.1, ...), custom_call_target="tpu_custom_call" | custom-call | tf_op jit(solution)/shard_map/attend/pallas_call | solution.py:360
  40.8 0.8 %store.1 = (bf16[1,32,2048]{2,1,0:T(8,128)(2,1)}, bf16[1,128,512]{2,1,0:T(8,128)(2,1)}, bf16[1,128,256]{2,1,0:T(8,128)(2,1)}, bf16[1,128,256]{2,1,0:T(8,128)(2,1)}) custom-call(bf16[1,32,2048]{2,1,0:T(8,128)(2,1)S(1)} %get-tuple-element.8.a_ref, bf16[1,128,512]{2,1,0:T(8,128)(2,1)S(1)} %get-tuple-element.9.b_ref, ...), custom_call_target="tpu_custom_call" | custom-call | tf_op jit(solution)/shard_map/store/pallas_call | solution.py:399

commit v3 on v2

--- a/solution.py
+++ b/solution.py
@@ -35,7 +35,7 @@
     kb0, kb1, kb2, kb3, kb4, vb0, vb1, vb2, vb3, vb4, qb, gb, flags,
     ks, vs, qs, gs, sc, dp, pb, dsb,
     ob, dqb, part, own, mate, near, far, hub, relay,
-    loc_sem, send_sem, rk_sem, rv_sem, rq_sem, rf_sem, out_sem, pd_sem, hub_sem,
+    loc_sem, late_sem, send_sem, rk_sem, rv_sem, rq_sem, rf_sem, out_sem, pd_sem, hub_sem,
 ):
     kb = (kb0, kb1, kb2, kb3, kb4)
     vb = (vb0, vb1, vb2, vb3, vb4)
@@ -67,28 +67,51 @@
     def greet(dev):
         pl.semaphore_signal(barrier, inc=1, device_id=dev, device_id_type=MESH)
 
-    greet((other, c, y))
-    met = 1
-    for d in range(1, NX):
+    inner = jnp.logical_not(first)
+    onward = jnp.logical_not(final)
+    skip_on = (x >= NX // 2) & onward
+    skip_back = (x < NX // 2) & inner
+
+    latest = (p == 0) & (c == 0) & (y == 0)
+    by_latest = jnp.logical_not(latest) & (((y == 0) & (c <= NX)) | (c == 0))
+
+    @pl.when(jnp.logical_not(latest))
+    def _():
+        greet((other, c, y))
         for j in range(2):
-            greet((j, c - x + lax.rem(x + d, NX), y))
-            met += 1
-    for d in range(1, n_tp):
+            for d in range(1, NX):
+                greet((j, c - x + lax.rem(x + d, NX), y))
+            for d in range(1, n_tp):
+                greet((j, c, lax.rem(y + d, n_tp)))
+        for cond, dev in (
+            (onward, ahead),
+            (inner, behind),
+            (skip_on, lax.rem(c + 2, n_ctx)),
+            (skip_back, lax.rem(c + n_ctx - 2, n_ctx)),
+        ):
+            @pl.when(cond)
+            def _():
+                for j in range(2):
+                    greet((j, dev, y))
+
+    met = 1 + 2 * (NX - 1) + 2 * (n_tp - 1) - by_latest.astype(jnp.int32)
+    for cond in (onward, inner, skip_on, skip_back):
+        met = met + 2 * cond.astype(jnp.int32)
+    pl.semaphore_wait(barrier, met)
+
+    @pl.when(latest)
+    def _():
+        beside = [(1, 0, 0)]
         for j in range(2):
-            greet((j, c, lax.rem(y + d, n_tp)))
-            met += 1
-
-    @pl.when(jnp.logical_not(final))
-    def _():
-        for j in range(2):
-            greet((j, ahead, y))
-
-    @pl.when(jnp.logical_not(first))
-    def _():
-        for j in range(2):
-            greet((j, behind, y))
-
-    pl.semaphore_wait(barrier, met + 2 * (1 - first.astype(jnp.int32)) + 2 * (1 - final.astype(jnp.int32)))
+            beside += [(j, d, 0) for d in range(1, min(NX + 1, n_ctx))]
+            beside += [(j, 0, t) for t in range(1, n_tp)]
+        for dev in beside:
+            pl.semaphore_signal(late_sem, inc=1, device_id=dev, device_id_type=MESH)
+
+    def meet_latest(cond):
+        @pl.when(by_latest & cond)
+        def _():
+            pl.semaphore_wait(late_sem, 1)
 
     count = [0]
     waits = []
@@ -118,25 +141,35 @@
                 pltpu.make_async_copy(ref, ref, sem).wait()
 
     mine = (other, c, y)
-    inner = jnp.logical_not(first)
-    onward = jnp.logical_not(final)
-    for j in range(2):
-        remote(cols(k_ref, j, HD), kb4.at[p], rk_sem.at[4], (j, ahead, y), onward)
+
+    def later(d):
+        return lax.rem(c + d, n_ctx)
+
+    def earlier(d):
+        return lax.rem(c + n_ctx - d, n_ctx)
+
+    def reaches(d):
+        return c + 2 < n_ctx if d == 2 else onward if d == REACH else x + d < NX
+
+    for d in (4, 1, 3, 2):
+        remote(swap_ref.at[0], flags.at[d], rf_sem.at[d], (p, later(d), y), reaches(d))
+    for src, dst, sem, d in (
+        (k_ref, kb, rk_sem, 4),
+        (k_ref, kb, rk_sem, 1),
+        (k_ref, kb, rk_sem, 3),
+        (v_ref, vb, rv_sem, 4),
+        (k_ref, kb, rk_sem, 2),
+        (v_ref, vb, rv_sem, 1),
+        (v_ref, vb, rv_sem, 3),
+        (v_ref, vb, rv_sem, 2),
+    ):
+        for j in range(2):
+            remote(cols(src, j, HD), dst[d].at[p], sem.at[d], (j, later(d), y), reaches(d))
+    meet_latest((y == 0) & (c == 0))
+    remote(cols(q_ref, other, QW), qb.at[p], rq_sem.at[0], mine)
     remote(cols(k_ref, other, HD), kb0.at[p], rk_sem.at[0], mine)
-    remote(cols(q_ref, other, QW), qb.at[p], rq_sem.at[0], mine)
-    for d in (2, 1, 3):
-        for j in range(2):
-            remote(cols(k_ref, j, HD), kb[d].at[p], rk_sem.at[d], (j, lax.rem(c + d, n_ctx), y), x + d < NX)
     remote(cols(g_ref, other, QW), gb.at[p], rq_sem.at[1], mine)
-    for j in range(2):
-        remote(cols(v_ref, j, HD), vb4.at[p], rv_sem.at[4], (j, ahead, y), onward)
     remote(cols(v_ref, other, HD), vb0.at[p], rv_sem.at[0], mine)
-    for d in (2, 1, 3):
-        for j in range(2):
-            remote(cols(v_ref, j, HD), vb[d].at[p], rv_sem.at[d], (j, lax.rem(c + d, n_ctx), y), x + d < NX)
-    remote(swap_ref.at[0], flags.at[4], rf_sem.at[4], (p, ahead, y), onward)
-    for d in range(1, NX):
-        remote(swap_ref.at[0], flags.at[d], rf_sem.at[d], (p, lax.rem(c + d, n_ctx), y), x + d < NX)
 
     for d in range(1, REACH + 1):
         @pl.when(c < d)
@@ -196,30 +229,29 @@
     arrived(gb.at[other], rq_sem.at[1])
     stack(gb, gs, swapped)
 
-    def pass_on(buf, sem):
-        arrived(buf[4], sem.at[4], inner)
-        for e in (2, 1, 3):
-            remote(buf[4], buf[4 - e], sem.at[4 - e], (p, lax.rem(c + n_ctx - e, n_ctx), y), inner & (x >= e))
-
-    pass_on(kb, rk_sem)
-    arrived(flags.at[4], rf_sem.at[4], inner)
-    for e in range(1, NX):
-        remote(flags.at[4], flags.at[4 - e], rf_sem.at[4 - e], (p, lax.rem(c + n_ctx - e, n_ctx), y), inner & (x >= e))
+    def pass_on(src, dst, sem):
+        arrived(src, sem.at[4], inner)
+        for e in (1, 3):
+            remote(src, dst(4 - e), sem.at[4 - e], (p, earlier(e), y), inner & (x >= e))
+
+    pass_on(flags.at[4], lambda d: flags.at[d], rf_sem)
+    pass_on(kb[4], lambda d: kb[d], rk_sem)
     take(4)
-    pass_on(vb, rv_sem)
+    pass_on(vb[4], lambda d: vb[d], rv_sem)
     arrived(vb0.at[other], rv_sem.at[0])
     take_v(0)
     take_v(4)
-    for d in (1, 2, 3):
+    for d in (2, 1, 3):
         arrived(flags.at[d], rf_sem.at[d], c >= d)
         arrived(kb[d], rk_sem.at[d], c >= d)
         take(d)
 
     def give(s, d):
-        dev = lax.rem(c + n_ctx - d, n_ctx)
-        for pi in range(2):
-            remote(part.at[d, s, pi], near.at[d - 1, s, p], pd_sem.at[s, d], (pi, dev, y), x >= d)
-        remote(part.at[d, s], relay.at[NX - d - 1, s], hub_sem.at[s, NX - d], (p, c + NX - d, y), inner & (x < d))
+        direct = c >= 2 if d == 2 else x >= d
+        for pi in range(2):
+            remote(part.at[d, s, pi], near.at[d - 1, s, p], pd_sem.at[s, d], (pi, earlier(d), y), direct)
+        if d != 2:
+            remote(part.at[d, s], relay.at[NX - d - 1, s], hub_sem.at[s, NX - d], (p, c + NX - d, y), inner & (x < d))
 
     for pi in range(2):
         top = jnp.max(sc[pi, 0], axis=0, keepdims=True)
@@ -242,11 +274,12 @@
                 hub[1, pi] = dv
             else:
                 part[d, 1, pi] = dv.astype(jnp.bfloat16)
-    for d in (3, 2, 1):
+    meet_latest((y == 0) & (c > 0))
+    for d in (3, 1, 2):
         give(1, d)
     remote(own.at[1, other], mate.at[1], pd_sem.at[1, 0], mine)
 
-    for d in (1, 2, 3):
+    for d in (2, 1, 3):
         arrived(vb[d], rv_sem.at[d], c >= d)
         take_v(d)
     for pi in range(2):
@@ -262,14 +295,22 @@
                 hub[0, pi] = dk
             else:
                 part[d, 0, pi] = dk.astype(jnp.bfloat16)
-    for d in (3, 2, 1):
+    for d in (3, 1, 2):
         give(0, d)
     remote(own.at[0, other], mate.at[0], pd_sem.at[0, 0], mine)
 
+    for pi in range(2):
+        o = (mm(dsb[pi].reshape(-1, QL), ks[pi].reshape(-1, HD), TN) * SCALE).astype(jnp.bfloat16)
+        for r in range(REP):
+            dqb[pi, :, r * HD:(r + 1) * HD] = o[r * BLK:(r + 1) * BLK]
+    keep_q = pltpu.make_async_copy(dqb.at[p], cols(gq_ref, p, QW), loc_sem.at[6])
+    keep_q.start()
+    remote(dqb.at[other], cols(gq_ref, p, QW), out_sem.at[1], mine)
     for pi in range(2):
         o = mm(pb[pi].reshape(-1, QL), vs[pi].reshape(-1, HD), TN).astype(jnp.bfloat16)
         for r in range(REP):
             ob[pi, :, r * HD:(r + 1) * HD] = o[r * BLK:(r + 1) * BLK]
+    meet_latest(y > 0)
     share = BLK // n_tp
     width = REP * HD
     at = pl.ds(pl.multiple_of((y * 2 + p) * width, width), width)
@@ -283,16 +324,9 @@
                 keep.start()
             else:
                 remote(ob.at[pi, rows], ao_ref.at[0, :, at], out_sem.at[0], (pi, c, t))
-    for pi in range(2):
-        o = (mm(dsb[pi].reshape(-1, QL), ks[pi].reshape(-1, HD), TN) * SCALE).astype(jnp.bfloat16)
-        for r in range(REP):
-            dqb[pi, :, r * HD:(r + 1) * HD] = o[r * BLK:(r + 1) * BLK]
-    keep_q = pltpu.make_async_copy(dqb.at[p], cols(gq_ref, p, QW), loc_sem.at[6])
-    keep_q.start()
-    remote(dqb.at[other], cols(gq_ref, p, QW), out_sem.at[1], mine)
 
     for s in (1, 0):
-        for e in range(1, NX):
+        for e in (1, 3):
             @pl.when(inner & (x >= e))
             def _():
                 arrived(relay.at[e - 1, s], hub_sem.at[s, e])
@@ -306,7 +340,7 @@
     for s, out in ((1, gv_ref), (0, gk_ref)):
         arrived(mate.at[s], pd_sem.at[s, 0])
         for d in range(1, NX):
-            @pl.when(x + d < NX)
+            @pl.when(reaches(d))
             def _():
                 arrived(near.at[d - 1, s], pd_sem.at[s, d])
                 own[s, p] = own[s, p] + near[d - 1, s, p].astype(jnp.float32)
@@ -384,6 +418,7 @@
             pltpu.VMEM((2, 2, BLK, HD), f32),
             pltpu.VMEM((3, 2, 2, BLK, HD), bf),
             dma((7,)),
+            pltpu.SemaphoreType.REGULAR,
             dma((80,)),
             dma((nd,)),
             dma((nd,)),

time: 41.8 us -> 33 us (0.79)
  the two profiles are of different devices: /device:TPU:5 before, /device:TPU:227 now
where the time goes in v3:
time: 33 us; the launch traced here: 32.8 us
  Pallas kernels  31.5 us (95%)
  between operations  1.29 us (4%)
    pallas_call x1, Pallas kernels, body(): pl.pallas_call(functools.partial(kernel, n_ctx, n_tp), out_shape=tuple((p...  30.8 us
    pallas_call x1, Pallas kernels, body(): pl.pallas_call(store, out_shape=tuple((jax.ShapeDtypeStruct(*item) for it...  0.77 us

profile of v3, /device:TPU:227, one launch (start us, length us, event | category | flops | bytes accessed | tf_op | source)
XLA Modules:
  0.0 32.8 jit_solution(12748361280425620444)
XLA Ops:
  1.3 30.8 %attend.1 = (bf16[1,32,2048]{2,1,0:T(8,128)(2,1)S(1)}, bf16[1,128,512]{2,1,0:T(8,128)(2,1)S(1)}, bf16[1,128,256]{2,1,0:T(8,128)(2,1)S(1)}, bf16[1,128,256]{2,1,0:T(8,128)(2,1)S(1)}) custom-call(bf16[1,128,512]{2,1,0:T(8,128)(2,1)} %q_ref.1, bf16[1,128,256]{2,1,0:T(8,128)(2,1)} %k_ref.1, bf16[1,128,256]{2,1,0:T(8,128)(2,1)} %v_ref.1, ...), custom_call_target="tpu_custom_call" | custom-call | tf_op jit(solution)/shard_map/attend/pallas_call | solution.py:394
  32.1 0.8 %store.1 = (bf16[1,32,2048]{2,1,0:T(8,128)(2,1)}, bf16[1,128,512]{2,1,0:T(8,128)(2,1)}, bf16[1,128,256]{2,1,0:T(8,128)(2,1)}, bf16[1,128,256]{2,1,0:T(8,128)(2,1)}) custom-call(bf16[1,32,2048]{2,1,0:T(8,128)(2,1)S(1)} %get-tuple-element.8.a_ref, bf16[1,128,512]{2,1,0:T(8,128)(2,1)S(1)} %get-tuple-element.9.b_ref, ...), custom_call_target="tpu_custom_call" | custom-call | tf_op jit(solution)/shard_map/store/pallas_call | solution.py:434

commit v4 on v3

--- a/solution.py
+++ b/solution.py
@@ -35,7 +35,7 @@
     kb0, kb1, kb2, kb3, kb4, vb0, vb1, vb2, vb3, vb4, qb, gb, flags,
     ks, vs, qs, gs, sc, dp, pb, dsb,
     ob, dqb, part, own, mate, near, far, hub, relay,
-    loc_sem, late_sem, send_sem, rk_sem, rv_sem, rq_sem, rf_sem, out_sem, pd_sem, hub_sem,
+    loc_sem, rk4_sem, rv4_sem, late_sem, send_sem, rk_sem, rv_sem, rq_sem, rf_sem, out_sem, pd_sem, hub_sem,
 ):
     kb = (kb0, kb1, kb2, kb3, kb4)
     vb = (vb0, vb1, vb2, vb3, vb4)
@@ -61,6 +61,7 @@
     ]
     for cp in local:
         cp.start()
+    flags[0, 0] = swap_ref[0, 0]
 
     barrier = pltpu.get_barrier_semaphore()
 
@@ -152,19 +153,25 @@
         return c + 2 < n_ctx if d == 2 else onward if d == REACH else x + d < NX
 
     for d in (4, 1, 3, 2):
-        remote(swap_ref.at[0], flags.at[d], rf_sem.at[d], (p, later(d), y), reaches(d))
-    for src, dst, sem, d in (
-        (k_ref, kb, rk_sem, 4),
-        (k_ref, kb, rk_sem, 1),
-        (k_ref, kb, rk_sem, 3),
-        (v_ref, vb, rv_sem, 4),
-        (k_ref, kb, rk_sem, 2),
-        (v_ref, vb, rv_sem, 1),
-        (v_ref, vb, rv_sem, 3),
-        (v_ref, vb, rv_sem, 2),
-    ):
+        remote(flags.at[0], flags.at[d], rf_sem.at[d], (p, later(d), y), reaches(d))
+    def send(pieces):
+        for src, dst, sem, d in pieces:
+            for j in range(2):
+                remote(cols(src, j, HD), dst[d].at[p], sem.at[d], (j, later(d), y), reaches(d))
+
+    def send_half(src, dst, sem, h):
+        rows = pl.ds(h * (BLK // 2), BLK // 2)
         for j in range(2):
-            remote(cols(src, j, HD), dst[d].at[p], sem.at[d], (j, later(d), y), reaches(d))
+            remote(
+                src.at[0, rows, pl.ds(j * HD, HD)], dst.at[p, rows], sem.at[h], (j, ahead, y), onward,
+            )
+
+    send_half(k_ref, kb4, rk4_sem, 0)
+    send_half(k_ref, kb4, rk4_sem, 1)
+    send([(k_ref, kb, rk_sem, 1), (k_ref, kb, rk_sem, 3)])
+    send_half(v_ref, vb4, rv4_sem, 0)
+    send_half(v_ref, vb4, rv4_sem, 1)
+    send([(k_ref, kb, rk_sem, 2), (v_ref, vb, rv_sem, 1), (v_ref, vb, rv_sem, 3), (v_ref, vb, rv_sem, 2)])
     meet_latest((y == 0) & (c == 0))
     remote(cols(q_ref, other, QW), qb.at[p], rq_sem.at[0], mine)
     remote(cols(k_ref, other, HD), kb0.at[p], rk_sem.at[0], mine)
@@ -234,10 +241,20 @@
         for e in (1, 3):
             remote(src, dst(4 - e), sem.at[4 - e], (p, earlier(e), y), inner & (x >= e))
 
+    def pass_halves(buf, sem, own_sem):
+        for h in range(2):
+            rows = pl.ds(h * (BLK // 2), BLK // 2)
+            arrived(buf[4].at[:, rows], own_sem.at[h], inner)
+            for e in (1, 3):
+                remote(
+                    buf[4].at[:, rows], buf[4 - e].at[:, rows], sem.at[4 - e],
+                    (p, earlier(e), y), inner & (x >= e),
+                )
+
     pass_on(flags.at[4], lambda d: flags.at[d], rf_sem)
-    pass_on(kb[4], lambda d: kb[d], rk_sem)
+    pass_halves(kb, rk_sem, rk4_sem)
     take(4)
-    pass_on(vb[4], lambda d: vb[d], rv_sem)
+    pass_halves(vb, rv_sem, rv4_sem)
     arrived(vb0.at[other], rv_sem.at[0])
     take_v(0)
     take_v(4)
@@ -246,13 +263,16 @@
         arrived(kb[d], rk_sem.at[d], c >= d)
         take(d)
 
-    def give(s, d):
+    def give(s, d, pi):
         direct = c >= 2 if d == 2 else x >= d
-        for pi in range(2):
-            remote(part.at[d, s, pi], near.at[d - 1, s, p], pd_sem.at[s, d], (pi, earlier(d), y), direct)
+        remote(part.at[d, s, pi], near.at[d - 1, s, p], pd_sem.at[s, d], (pi, earlier(d), y), direct)
         if d != 2:
-            remote(part.at[d, s], relay.at[NX - d - 1, s], hub_sem.at[s, NX - d], (p, c + NX - d, y), inner & (x < d))
-
+            remote(
+                part.at[d, s, pi], relay.at[NX - d - 1, s, pi], hub_sem.at[s, pi, NX - d],
+                (p, c + NX - d, y), inner & (x < d),
+            )
+
+    meet_latest((y == 0) & (c > 0))
     for pi in range(2):
         top = jnp.max(sc[pi, 0], axis=0, keepdims=True)
         for d in range(1, REACH + 1):
@@ -263,7 +283,7 @@
             sc[pi, d] = e
             total = total + jnp.sum(e, axis=0, keepdims=True)
         inv = 1.0 / total
-        for d in (3, 2, 1, 4, 0):
+        for d in (3, 1, 2, 4, 0):
             pr = sc[pi, d] * inv
             sc[pi, d] = pr
             pb[pi, d] = pr.astype(jnp.bfloat16)
@@ -274,9 +294,10 @@
                 hub[1, pi] = dv
             else:
                 part[d, 1, pi] = dv.astype(jnp.bfloat16)
-    meet_latest((y == 0) & (c > 0))
-    for d in (3, 1, 2):
-        give(1, d)
+        for d in (3, 1):
+            give(1, d, pi)
+    for pi in range(2):
+        give(1, 2, pi)
     remote(own.at[1, other], mate.at[1], pd_sem.at[1, 0], mine)
 
     for d in (2, 1, 3):
@@ -286,7 +307,7 @@
         delta = jnp.zeros((1, QL), jnp.float32)
         for d in range(REACH + 1):
             delta = delta + jnp.sum(sc[pi, d] * dp[pi, d], axis=0, keepdims=True)
-        for d in (3, 2, 1, 4, 0):
+        for d in (3, 1, 2, 4, 0):
             dsb[pi, d] = (sc[pi, d] * (dp[pi, d] - delta)).astype(jnp.bfloat16)
             dk = mm(dsb[pi, d], qs[pi], NN) * SCALE
             if d == 0:
@@ -295,8 +316,10 @@
                 hub[0, pi] = dk
             else:
                 part[d, 0, pi] = dk.astype(jnp.bfloat16)
-    for d in (3, 1, 2):
-        give(0, d)
+        for d in (3, 1):
+            give(0, d, pi)
+    for pi in range(2):
+        give(0, 2, pi)
     remote(own.at[0, other], mate.at[0], pd_sem.at[0, 0], mine)
 
     for pi in range(2):
@@ -326,15 +349,13 @@
                 remote(ob.at[pi, rows], ao_ref.at[0, :, at], out_sem.at[0], (pi, c, t))
 
     for s in (1, 0):
-        for e in (1, 3):
-            @pl.when(inner & (x >= e))
-            def _():
-                arrived(relay.at[e - 1, s], hub_sem.at[s, e])
-                for pi in range(2):
+        for pi in range(2):
+            for e in (1, 3):
+                @pl.when(inner & (x >= e))
+                def _():
+                    arrived(relay.at[e - 1, s, pi], hub_sem.at[s, pi, e])
                     hub[s, pi] = hub[s, pi] + relay[e - 1, s, pi].astype(jnp.float32)
-        for pi in range(2):
             part[4, s, pi] = hub[s, pi].astype(jnp.bfloat16)
-        for pi in range(2):
             remote(part.at[4, s, pi], far.at[s, p], pd_sem.at[s, 4], (pi, behind, y), inner)
 
     for s, out in ((1, gv_ref), (0, gk_ref)):
@@ -418,15 +439,17 @@
             pltpu.VMEM((2, 2, BLK, HD), f32),
             pltpu.VMEM((3, 2, 2, BLK, HD), bf),
             dma((7,)),
+            dma((2,)),
+            dma((2,)),
             pltpu.SemaphoreType.REGULAR,
-            dma((80,)),
+            dma((100,)),
             dma((nd,)),
             dma((nd,)),
             dma((2,)),
             dma((nd,)),
             dma((2,)),
             dma((2, nd)),
-            dma((2, NX)),
+            dma((2, 2, NX)),
         ],
         compiler_params=pltpu.CompilerParams(collective_id=0, has_side_effects=True),
         name="attend",

time: 33 us -> 32.5 us (0.985)
  the two profiles are of different devices: /device:TPU:227 before, /device:TPU:3 now
where the time goes in v4:
time: 32.5 us; the launch traced here: 32.3 us
  Pallas kernels  31 us (95%)
  between operations  1.29 us (4%)
    pallas_call x1, Pallas kernels, body(): pl.pallas_call(functools.partial(kernel, n_ctx, n_tp), out_shape=tuple((p...  30.2 us
    pallas_call x1, Pallas kernels, body(): pl.pallas_call(store, out_shape=tuple((jax.ShapeDtypeStruct(*item) for it...  0.77 us

profile of v4, /device:TPU:3, one launch (start us, length us, event | category | flops | bytes accessed | tf_op | source)
XLA Modules:
  0.0 32.3 jit_solution(12208267497497622483)
XLA Ops:
  1.3 30.2 %attend.1 = (bf16[1,32,2048]{2,1,0:T(8,128)(2,1)S(1)}, bf16[1,128,512]{2,1,0:T(8,128)(2,1)S(1)}, bf16[1,128,256]{2,1,0:T(8,128)(2,1)S(1)}, bf16[1,128,256]{2,1,0:T(8,128)(2,1)S(1)}) custom-call(bf16[1,128,512]{2,1,0:T(8,128)(2,1)} %q_ref.1, bf16[1,128,256]{2,1,0:T(8,128)(2,1)} %k_ref.1, bf16[1,128,256]{2,1,0:T(8,128)(2,1)} %v_ref.1, ...), custom_call_target="tpu_custom_call" | custom-call | tf_op jit(solution)/shard_map/attend/pallas_call | solution.py:415
  31.5 0.8 %store.1 = (bf16[1,32,2048]{2,1,0:T(8,128)(2,1)}, bf16[1,128,512]{2,1,0:T(8,128)(2,1)}, bf16[1,128,256]{2,1,0:T(8,128)(2,1)}, bf16[1,128,256]{2,1,0:T(8,128)(2,1)}) custom-call(bf16[1,32,2048]{2,1,0:T(8,128)(2,1)S(1)} %get-tuple-element.8.a_ref, bf16[1,128,512]{2,1,0:T(8,128)(2,1)S(1)} %get-tuple-element.9.b_ref, ...), custom_call_target="tpu_custom_call" | custom-call | tf_op jit(solution)/shard_map/store/pallas_call | solution.py:457

commit v5 on v4

--- a/solution.py
+++ b/solution.py
@@ -72,6 +72,8 @@
     onward = jnp.logical_not(final)
     skip_on = (x >= NX // 2) & onward
     skip_back = (x < NX // 2) & inner
+    side_on = (x == 1) & onward
+    side_back = (x == 0) & inner
 
     latest = (p == 0) & (c == 0) & (y == 0)
     by_latest = jnp.logical_not(latest) & (((y == 0) & (c <= NX)) | (c == 0))
@@ -89,6 +91,8 @@
             (inner, behind),
             (skip_on, lax.rem(c + 2, n_ctx)),
             (skip_back, lax.rem(c + n_ctx - 2, n_ctx)),
+            (side_on, lax.rem(c + 3, n_ctx)),
+            (side_back, lax.rem(c + n_ctx - 3, n_ctx)),
         ):
             @pl.when(cond)
             def _():
@@ -96,7 +100,7 @@
                     greet((j, dev, y))
 
     met = 1 + 2 * (NX - 1) + 2 * (n_tp - 1) - by_latest.astype(jnp.int32)
-    for cond in (onward, inner, skip_on, skip_back):
+    for cond in (onward, inner, skip_on, skip_back, side_on, side_back):
         met = met + 2 * cond.astype(jnp.int32)
     pl.semaphore_wait(barrier, met)
 
@@ -152,12 +156,18 @@
     def reaches(d):
         return c + 2 < n_ctx if d == 2 else onward if d == REACH else x + d < NX
 
+    def starts(d):
+        return (x == 0) | side_on if d == 3 else reaches(d)
+
     for d in (4, 1, 3, 2):
-        remote(flags.at[0], flags.at[d], rf_sem.at[d], (p, later(d), y), reaches(d))
-    def send(pieces):
+        remote(flags.at[0], flags.at[d], rf_sem.at[d], (p, later(d), y), starts(d))
+    def send(pieces, cond=None):
         for src, dst, sem, d in pieces:
             for j in range(2):
-                remote(cols(src, j, HD), dst[d].at[p], sem.at[d], (j, later(d), y), reaches(d))
+                remote(
+                    cols(src, j, HD), dst[d].at[p], sem.at[d], (j, later(d), y),
+                    starts(d) if cond is None else cond,
+                )
 
     def send_half(src, dst, sem, h):
         rows = pl.ds(h * (BLK // 2), BLK // 2)
@@ -171,7 +181,9 @@
     send([(k_ref, kb, rk_sem, 1), (k_ref, kb, rk_sem, 3)])
     send_half(v_ref, vb4, rv4_sem, 0)
     send_half(v_ref, vb4, rv4_sem, 1)
-    send([(k_ref, kb, rk_sem, 2), (v_ref, vb, rv_sem, 1), (v_ref, vb, rv_sem, 3), (v_ref, vb, rv_sem, 2)])
+    send([(k_ref, kb, rk_sem, 2)], x < NX // 2)
+    send([(v_ref, vb, rv_sem, 1), (v_ref, vb, rv_sem, 3)])
+    send([(v_ref, vb, rv_sem, 2)], x < NX // 2)
     meet_latest((y == 0) & (c == 0))
     remote(cols(q_ref, other, QW), qb.at[p], rq_sem.at[0], mine)
     remote(cols(k_ref, other, HD), kb0.at[p], rk_sem.at[0], mine)
@@ -236,32 +248,39 @@
     arrived(gb.at[other], rq_sem.at[1])
     stack(gb, gs, swapped)
 
-    def pass_on(src, dst, sem):
-        arrived(src, sem.at[4], inner)
-        for e in (1, 3):
-            remote(src, dst(4 - e), sem.at[4 - e], (p, earlier(e), y), inner & (x >= e))
+    relays = inner & (x >= 2)
 
     def pass_halves(buf, sem, own_sem):
         for h in range(2):
             rows = pl.ds(h * (BLK // 2), BLK // 2)
-            arrived(buf[4].at[:, rows], own_sem.at[h], inner)
-            for e in (1, 3):
+            arrived(buf[4].at[:, rows], own_sem.at[h], relays)
+            for e in (3, 1):
                 remote(
                     buf[4].at[:, rows], buf[4 - e].at[:, rows], sem.at[4 - e],
-                    (p, earlier(e), y), inner & (x >= e),
+                    (p, earlier(e), y), inner & (x >= max(e, 2)),
                 )
-
-    pass_on(flags.at[4], lambda d: flags.at[d], rf_sem)
+            if h == 0 and own_sem is rk4_sem:
+                send([(k_ref, kb, rk_sem, 2), (v_ref, vb, rv_sem, 2)], skip_on)
+
+    def last_halves(buf, own_sem):
+        for h in range(2):
+            rows = pl.ds(h * (BLK // 2), BLK // 2)
+            arrived(buf[4].at[:, rows], own_sem.at[h], inner & (x < 2))
+
+    arrived(flags.at[4], rf_sem.at[4], relays)
+    for e in (1, 3):
+        remote(flags.at[4], flags.at[4 - e], rf_sem.at[4 - e], (p, earlier(e), y), inner & (x >= max(e, 2)))
     pass_halves(kb, rk_sem, rk4_sem)
-    take(4)
     pass_halves(vb, rv_sem, rv4_sem)
     arrived(vb0.at[other], rv_sem.at[0])
     take_v(0)
-    take_v(4)
-    for d in (2, 1, 3):
+    for d in (2, 3, 1):
         arrived(flags.at[d], rf_sem.at[d], c >= d)
         arrived(kb[d], rk_sem.at[d], c >= d)
         take(d)
+    arrived(flags.at[4], rf_sem.at[4], inner & (x < 2))
+    last_halves(kb, rk4_sem)
+    take(4)
 
     def give(s, d, pi):
         direct = c >= 2 if d == 2 else x >= d
@@ -271,6 +290,12 @@
                 part.at[d, s, pi], relay.at[NX - d - 1, s, pi], hub_sem.at[s, pi, NX - d],
                 (p, c + NX - d, y), inner & (x < d),
             )
+
+    def hand_back(s, pi, cond):
+        @pl.when(cond)
+        def _():
+            part[4, s, pi] = hub[s, pi].astype(jnp.bfloat16)
+        remote(part.at[4, s, pi], far.at[s, p], pd_sem.at[s, 4], (pi, behind, y), inner & cond)
 
     meet_latest((y == 0) & (c > 0))
     for pi in range(2):
@@ -283,7 +308,7 @@
             sc[pi, d] = e
             total = total + jnp.sum(e, axis=0, keepdims=True)
         inv = 1.0 / total
-        for d in (3, 1, 2, 4, 0):
+        for d in (1, 3, 2, 4, 0):
             pr = sc[pi, d] * inv
             sc[pi, d] = pr
             pb[pi, d] = pr.astype(jnp.bfloat16)
@@ -294,20 +319,23 @@
                 hub[1, pi] = dv
             else:
                 part[d, 1, pi] = dv.astype(jnp.bfloat16)
-        for d in (3, 1):
+        for d in (1, 3):
             give(1, d, pi)
+        hand_back(1, pi, x < 1)
     for pi in range(2):
         give(1, 2, pi)
     remote(own.at[1, other], mate.at[1], pd_sem.at[1, 0], mine)
 
-    for d in (2, 1, 3):
+    for d in (2, 3, 1):
         arrived(vb[d], rv_sem.at[d], c >= d)
         take_v(d)
+    last_halves(vb, rv4_sem)
+    take_v(4)
     for pi in range(2):
         delta = jnp.zeros((1, QL), jnp.float32)
         for d in range(REACH + 1):
             delta = delta + jnp.sum(sc[pi, d] * dp[pi, d], axis=0, keepdims=True)
-        for d in (3, 1, 2, 4, 0):
+        for d in (1, 3, 2, 4, 0):
             dsb[pi, d] = (sc[pi, d] * (dp[pi, d] - delta)).astype(jnp.bfloat16)
             dk = mm(dsb[pi, d], qs[pi], NN) * SCALE
             if d == 0:
@@ -316,10 +344,9 @@
                 hub[0, pi] = dk
             else:
                 part[d, 0, pi] = dk.astype(jnp.bfloat16)
-        for d in (3, 1):
+        for d in (1, 3):
             give(0, d, pi)
-    for pi in range(2):
-        give(0, 2, pi)
+        hand_back(0, pi, x < 1)
     remote(own.at[0, other], mate.at[0], pd_sem.at[0, 0], mine)
 
     for pi in range(2):
@@ -348,6 +375,9 @@
             else:
                 remote(ob.at[pi, rows], ao_ref.at[0, :, at], out_sem.at[0], (pi, c, t))
 
+    for pi in range(2):
+        give(0, 2, pi)
+
     for s in (1, 0):
         for pi in range(2):
             for e in (1, 3):
@@ -355,8 +385,7 @@
                 def _():
                     arrived(relay.at[e - 1, s, pi], hub_sem.at[s, pi, e])
                     hub[s, pi] = hub[s, pi] + relay[e - 1, s, pi].astype(jnp.float32)
-            part[4, s, pi] = hub[s, pi].astype(jnp.bfloat16)
-            remote(part.at[4, s, pi], far.at[s, p], pd_sem.at[s, 4], (pi, behind, y), inner)
+            hand_back(s, pi, x >= 1)
 
     for s, out in ((1, gv_ref), (0, gk_ref)):
         arrived(mate.at[s], pd_sem.at[s, 0])

time: 32.5 us -> 32.4 us (level)
  the two profiles are of different devices: /device:TPU:3 before, /device:TPU:491 now
where the time goes in v5:
time: 32.4 us; the launch traced here: 32.2 us
  Pallas kernels  30.9 us (95%)
  between operations  1.29 us (4%)
    pallas_call x1, Pallas kernels, body(): pl.pallas_call(functools.partial(kernel, n_ctx, n_tp), out_shape=tuple((p...  30.2 us
    pallas_call x1, Pallas kernels, body(): pl.pallas_call(store, out_shape=tuple((jax.ShapeDtypeStruct(*item) for it...  0.77 us

profile of v5, /device:TPU:491, one launch (start us, length us, event | category | flops | bytes accessed | tf_op | source)
XLA Modules:
  0.0 32.2 jit_solution(4926845256484147061)
XLA Ops:
  1.3 30.2 %attend.1 = (bf16[1,32,2048]{2,1,0:T(8,128)(2,1)S(1)}, bf16[1,128,512]{2,1,0:T(8,128)(2,1)S(1)}, bf16[1,128,256]{2,1,0:T(8,128)(2,1)S(1)}, bf16[1,128,256]{2,1,0:T(8,128)(2,1)S(1)}) custom-call(bf16[1,128,512]{2,1,0:T(8,128)(2,1)} %q_ref.1, bf16[1,128,256]{2,1,0:T(8,128)(2,1)} %k_ref.1, bf16[1,128,256]{2,1,0:T(8,128)(2,1)} %v_ref.1, ...), custom_call_target="tpu_custom_call" | custom-call | tf_op jit(solution)/shard_map/attend/pallas_call | solution.py:444
  31.5 0.8 %store.1 = (bf16[1,32,2048]{2,1,0:T(8,128)(2,1)}, bf16[1,128,512]{2,1,0:T(8,128)(2,1)}, bf16[1,128,256]{2,1,0:T(8,128)(2,1)}, bf16[1,128,256]{2,1,0:T(8,128)(2,1)}) custom-call(bf16[1,32,2048]{2,1,0:T(8,128)(2,1)S(1)} %get-tuple-element.8.a_ref, bf16[1,128,512]{2,1,0:T(8,128)(2,1)S(1)} %get-tuple-element.9.b_ref, ...), custom_call_target="tpu_custom_call" | custom-call | tf_op jit(solution)/shard_map/store/pallas_call | solution.py:486

commit v6 on v5

--- a/solution.py
+++ b/solution.py
@@ -74,6 +74,8 @@
     skip_back = (x < NX // 2) & inner
     side_on = (x == 1) & onward
     side_back = (x == 0) & inner
+    wrap_on = (x == NX - 1) & onward
+    third_back = (x == 2) & inner
 
     latest = (p == 0) & (c == 0) & (y == 0)
     by_latest = jnp.logical_not(latest) & (((y == 0) & (c <= NX)) | (c == 0))
@@ -93,6 +95,10 @@
             (skip_back, lax.rem(c + n_ctx - 2, n_ctx)),
             (side_on, lax.rem(c + 3, n_ctx)),
             (side_back, lax.rem(c + n_ctx - 3, n_ctx)),
+            (wrap_on, lax.rem(c + 1, n_ctx)),
+            (wrap_on, lax.rem(c + 3, n_ctx)),
+            (third_back, lax.rem(c + n_ctx - 3, n_ctx)),
+            (side_back, lax.rem(c + n_ctx - 1, n_ctx)),
         ):
             @pl.when(cond)
             def _():
@@ -100,7 +106,7 @@
                     greet((j, dev, y))
 
     met = 1 + 2 * (NX - 1) + 2 * (n_tp - 1) - by_latest.astype(jnp.int32)
-    for cond in (onward, inner, skip_on, skip_back, side_on, side_back):
+    for cond in (onward, inner, skip_on, skip_back, side_on, side_back, wrap_on, side_back, wrap_on, third_back):
         met = met + 2 * cond.astype(jnp.int32)
     pl.semaphore_wait(barrier, met)
 
@@ -283,12 +289,15 @@
     take(4)
 
     def give(s, d, pi):
-        direct = c >= 2 if d == 2 else x >= d
+        straight = d == 1 and s == 0
+        direct = c >= d if d == 2 or straight else x >= d
+        if d == 3 and s == 0:
+            direct = direct | third_back
         remote(part.at[d, s, pi], near.at[d - 1, s, p], pd_sem.at[s, d], (pi, earlier(d), y), direct)
-        if d != 2:
+        if d == 3 or (d == 1 and not straight):
             remote(
                 part.at[d, s, pi], relay.at[NX - d - 1, s, pi], hub_sem.at[s, pi, NX - d],
-                (p, c + NX - d, y), inner & (x < d),
+                (p, c + NX - d, y), inner & (x < (2 if s == 0 else d)),
             )
 
     def hand_back(s, pi, cond):
@@ -346,7 +355,7 @@
                 part[d, 0, pi] = dk.astype(jnp.bfloat16)
         for d in (1, 3):
             give(0, d, pi)
-        hand_back(0, pi, x < 1)
+        hand_back(0, pi, (x == 0) | (x == NX - 1))
     remote(own.at[0, other], mate.at[0], pd_sem.at[0, 0], mine)
 
     for pi in range(2):
@@ -381,16 +390,19 @@
     for s in (1, 0):
         for pi in range(2):
             for e in (1, 3):
-                @pl.when(inner & (x >= e))
+                if s == 0 and e == 3:
+                    continue
+
+                @pl.when(inner & (x >= e) & (x < (NX - 1 if s == 0 else NX)))
                 def _():
                     arrived(relay.at[e - 1, s, pi], hub_sem.at[s, pi, e])
                     hub[s, pi] = hub[s, pi] + relay[e - 1, s, pi].astype(jnp.float32)
-            hand_back(s, pi, x >= 1)
+            hand_back(s, pi, (x >= 1) & (x < (NX - 1 if s == 0 else NX)))
 
     for s, out in ((1, gv_ref), (0, gk_ref)):
         arrived(mate.at[s], pd_sem.at[s, 0])
         for d in range(1, NX):
-            @pl.when(reaches(d))
+            @pl.when(reaches(d) | (wrap_on if d != 2 and s == 0 else reaches(d)))
             def _():
                 arrived(near.at[d - 1, s], pd_sem.at[s, d])
                 own[s, p] = own[s, p] + near[d - 1, s, p].astype(jnp.float32)

time: 32.4 us -> 32.4 us (level)
  the two profiles are of different devices: /device:TPU:491 before, /device:TPU:511 now
where the time goes in v6:
time: 32.4 us; the launch traced here: 32.2 us
  Pallas kernels  30.9 us (95%)
  between operations  1.29 us (4%)
    pallas_call x1, Pallas kernels, body(): pl.pallas_call(functools.partial(kernel, n_ctx, n_tp), out_shape=tuple((p...  30.1 us
    pallas_call x1, Pallas kernels, body(): pl.pallas_call(store, out_shape=tuple((jax.ShapeDtypeStruct(*item) for it...  0.77 us

profile of v6, /device:TPU:511, one launch (start us, length us, event | category | flops | bytes accessed | tf_op | source)
XLA Modules:
  0.0 32.2 jit_solution(8906569668884954561)
XLA Ops:
  1.3 30.1 %attend.1 = (bf16[1,32,2048]{2,1,0:T(8,128)(2,1)S(1)}, bf16[1,128,512]{2,1,0:T(8,128)(2,1)S(1)}, bf16[1,128,256]{2,1,0:T(8,128)(2,1)S(1)}, bf16[1,128,256]{2,1,0:T(8,128)(2,1)S(1)}) custom-call(bf16[1,128,512]{2,1,0:T(8,128)(2,1)} %q_ref.1, bf16[1,128,256]{2,1,0:T(8,128)(2,1)} %k_ref.1, bf16[1,128,256]{2,1,0:T(8,128)(2,1)} %v_ref.1, ...), custom_call_target="tpu_custom_call" | custom-call | tf_op jit(solution)/shard_map/attend/pallas_call | solution.py:456
  31.4 0.8 %store.1 = (bf16[1,32,2048]{2,1,0:T(8,128)(2,1)}, bf16[1,128,512]{2,1,0:T(8,128)(2,1)}, bf16[1,128,256]{2,1,0:T(8,128)(2,1)}, bf16[1,128,256]{2,1,0:T(8,128)(2,1)}) custom-call(bf16[1,32,2048]{2,1,0:T(8,128)(2,1)S(1)} %get-tuple-element.8.a_ref, bf16[1,128,512]{2,1,0:T(8,128)(2,1)S(1)} %get-tuple-element.9.b_ref, ...), custom_call_target="tpu_custom_call" | custom-call | tf_op jit(solution)/shard_map/store/pallas_call | solution.py:498

commit v7 on v6

--- a/solution.py
+++ b/solution.py
@@ -366,6 +366,8 @@
     keep_q.start()
     remote(dqb.at[other], cols(gq_ref, p, QW), out_sem.at[1], mine)
     for pi in range(2):
+        give(0, 2, pi)
+    for pi in range(2):
         o = mm(pb[pi].reshape(-1, QL), vs[pi].reshape(-1, HD), TN).astype(jnp.bfloat16)
         for r in range(REP):
             ob[pi, :, r * HD:(r + 1) * HD] = o[r * BLK:(r + 1) * BLK]
@@ -383,9 +385,6 @@
                 keep.start()
             else:
                 remote(ob.at[pi, rows], ao_ref.at[0, :, at], out_sem.at[0], (pi, c, t))
-
-    for pi in range(2):
-        give(0, 2, pi)
 
     for s in (1, 0):
         for pi in range(2):

time: 32.4 us -> 32.4 us (level)
  no operation moved by 1% of the time
where the time goes in v7:
time: 32.4 us; the launch traced here: 32.2 us
  Pallas kernels  30.9 us (95%)
  between operations  1.29 us (4%)
    pallas_call x1, Pallas kernels, body(): pl.pallas_call(functools.partial(kernel, n_ctx, n_tp), out_shape=tuple((p...  30.1 us
    pallas_call x1, Pallas kernels, body(): pl.pallas_call(store, out_shape=tuple((jax.ShapeDtypeStruct(*item) for it...  0.77 us

profile of v7, /device:TPU:511, one launch (start us, length us, event | category | flops | bytes accessed | tf_op | source)
XLA Modules:
  0.0 32.2 jit_solution(8154889602319048979)
XLA Ops:
  1.3 30.1 %attend.1 = (bf16[1,32,2048]{2,1,0:T(8,128)(2,1)S(1)}, bf16[1,128,512]{2,1,0:T(8,128)(2,1)S(1)}, bf16[1,128,256]{2,1,0:T(8,128)(2,1)S(1)}, bf16[1,128,256]{2,1,0:T(8,128)(2,1)S(1)}) custom-call(bf16[1,128,512]{2,1,0:T(8,128)(2,1)} %q_ref.1, bf16[1,128,256]{2,1,0:T(8,128)(2,1)} %k_ref.1, bf16[1,128,256]{2,1,0:T(8,128)(2,1)} %v_ref.1, ...), custom_call_target="tpu_custom_call" | custom-call | tf_op jit(solution)/shard_map/attend/pallas_call | solution.py:455
  31.4 0.8 %store.1 = (bf16[1,32,2048]{2,1,0:T(8,128)(2,1)}, bf16[1,128,512]{2,1,0:T(8,128)(2,1)}, bf16[1,128,256]{2,1,0:T(8,128)(2,1)}, bf16[1,128,256]{2,1,0:T(8,128)(2,1)}) custom-call(bf16[1,32,2048]{2,1,0:T(8,128)(2,1)S(1)} %get-tuple-element.8.a_ref, bf16[1,128,512]{2,1,0:T(8,128)(2,1)S(1)} %get-tuple-element.9.b_ref, ...), custom_call_target="tpu_custom_call" | custom-call | tf_op jit(solution)/shard_map/store/pallas_call | solution.py:497
